TPU v7x, 32 devices: a whole 2x2x4 slice. The times are simulated.
32 devices in a mesh: dp: 8 (over z, x), mp: 4 (over y, core).
Axes of the slice: x: 2, y: 2, z: 4, core: 2. Of those that a mesh axis runs over, the one named last changes fastest.
Arguments:
- tokens: bfloat16 [32768, 768], P('dp'), may hold values from -6 to 6
- segment: int32 [32768], P('dp'), may hold values from 0 to 8, as said below
- ln1_gain: bfloat16 [768], P('mp'), may hold values from 0.5 to 1.5
- ln1_bias: bfloat16 [768], P('mp'), may hold values from -2 to 2
- w_qkv: bfloat16 [3, 768, 768], P(None, None, 'mp'), may hold values from -0.21875 to 0.21875
- b_qv: bfloat16 [2, 768], P(None, 'mp'), may hold values from -2 to 2
- w_out: bfloat16 [768, 768], P('mp'), may hold values from -0.875 to 0.875
- b_out: bfloat16 [768], P('mp'), may hold values from -2 to 2
- ln2_gain: bfloat16 [768], P('mp'), may hold values from 0.5 to 1.5
- ln2_bias: bfloat16 [768], P('mp'), may hold values from -2 to 2
- w_up: bfloat16 [768, 3072], P(None, 'mp'), may hold values from -0.21875 to 0.21875
- b_up: bfloat16 [3072], P('mp'), may hold values from -3 to 3
- w_down: bfloat16 [3072, 768], P('mp'), may hold values from -0.109375 to 0.109375
- b_down: bfloat16 [768], P('mp'), may hold values from -2 to 2
- cotangent: bfloat16 [32768, 768], P(('dp', 'mp')), may hold values from -6 to 6
Outputs:
- output: bfloat16 [32768, 768], P(('dp', 'mp'))
- grad_x: float32 [32768, 768], P(('dp', 'mp'))
- grad_ln1_gain: float32 [768], P('mp')
- grad_ln1_bias: float32 [768], P('mp')
- grad_w_qkv: float32 [3, 768, 768], P(None, None, 'mp')
- grad_b_qv: float32 [2, 768], P(None, 'mp')
- grad_w_out: float32 [768, 768], P('mp')
- grad_b_out: float32 [768], P('mp')
- grad_ln2_gain: float32 [768], P('mp')
- grad_ln2_bias: float32 [768], P('mp')
- grad_w_up: float32 [768, 3072], P(None, 'mp')
- grad_b_up: float32 [3072], P('mp')
- grad_w_down: float32 [3072, 768], P('mp')
- grad_b_down: float32 [768], P('mp')
Inputs may be any that keep to these rules, and one draw needn't show every extreme that they name: `segment`: within each aligned sequence of 512 rows the numbers never fall except to 0; 0 marks padding rows, which stand at the end of a sequence.
All inputs are finite; a program needn't handle non-finite values.
Results may differ from a plain program's by a relative error of at most 0.018.
Values may be sent and summed in bfloat16 or wider, within the bound.
A program may use at most 256 MiB of HBM per device.

v0:
```python
import jax
import jax.numpy as jnp
from jax import lax
from jax.sharding import PartitionSpec as P

HD = 64
LEN = 512


def layer_norm(values, norm_gain, norm_shift):
    centered = values - jnp.mean(values, axis=-1, keepdims=True)
    spread = jnp.mean(centered * centered, axis=-1, keepdims=True)
    return centered * lax.rsqrt(spread + 1e-06) * norm_gain + norm_shift


def norm_back(values, norm_gain, norm_shift, incoming):
    result, pull_back = jax.vjp(layer_norm, values, norm_gain, norm_shift)
    return pull_back(incoming)


def gelu_exact(values):
    return jax.nn.gelu(values, approximate=False)


def gelu_back(values, incoming):
    result, pull_back = jax.vjp(gelu_exact, values)
    return pull_back(incoming)[0]


def plain_dot(left, right):
    return jnp.dot(left, right, preferred_element_type=jnp.float32)


def over_rows(left, right):
    return lax.dot_general(
        left, right, (((0,), (0,)), ((), ())), preferred_element_type=jnp.float32
    )


def against(left, right):
    return lax.dot_general(
        left, right, (((1,), (1,)), ((), ())), preferred_element_type=jnp.float32
    )


def allowed_pairs(segment):
    length = segment.shape[0]
    row_ids = lax.broadcasted_iota(jnp.int32, (length, length), 0)
    col_ids = lax.broadcasted_iota(jnp.int32, (length, length), 1)
    same = (segment[:, None] == segment[None, :]) & (segment[None, :] != 0)
    return same | (row_ids == col_ids)


def head_scores(query_heads, key_heads, segment):
    score_scale = query_heads.shape[-1] ** (-0.5)
    scores = (
        jnp.einsum("qhd,khd->hqk", query_heads, key_heads, preferred_element_type=jnp.float32)
        * score_scale
    )
    return jnp.where(allowed_pairs(segment)[None], scores, -1e30)


def attend_forward(entries):
    query_heads, key_heads, value_heads, segment = entries
    masked = head_scores(query_heads, key_heads, segment)
    row_max = jnp.max(masked, axis=-1, keepdims=True)
    expo_scores = jnp.exp(masked - row_max)
    row_sum = jnp.sum(expo_scores, axis=-1, keepdims=True)
    attn_probs = (expo_scores / row_sum).astype(jnp.bfloat16)
    attended = jnp.einsum(
        "hqk,khd->qhd", attn_probs, value_heads, preferred_element_type=jnp.float32
    )
    return (attended.astype(jnp.bfloat16), (row_max + jnp.log(row_sum))[..., 0])


def attend_backward(entries):
    query_heads, key_heads, value_heads, segment, log_total, grad_heads = entries
    score_scale = query_heads.shape[-1] ** (-0.5)
    attn_probs = jnp.exp(head_scores(query_heads, key_heads, segment) - log_total[..., None])
    grad_probs = jnp.einsum(
        "qhd,khd->hqk", grad_heads, value_heads, preferred_element_type=jnp.float32
    )
    inner = jnp.sum(attn_probs * grad_probs, axis=-1, keepdims=True)
    grad_scores = (attn_probs * (grad_probs - inner)).astype(jnp.bfloat16)
    grad_query = (
        jnp.einsum("hqk,khd->qhd", grad_scores, key_heads, preferred_element_type=jnp.float32)
        * score_scale
    )
    grad_key = (
        jnp.einsum("hqk,qhd->khd", grad_scores, query_heads, preferred_element_type=jnp.float32)
        * score_scale
    )
    grad_value = jnp.einsum(
        "hqk,qhd->khd",
        attn_probs.astype(jnp.bfloat16),
        grad_heads,
        preferred_element_type=jnp.float32,
    )
    return (
        grad_query.astype(jnp.bfloat16),
        grad_key.astype(jnp.bfloat16),
        grad_value.astype(jnp.bfloat16),
    )


def per_device(
    tokens,
    segment,
    ln1_gain,
    ln1_bias,
    w_qkv,
    b_qv,
    w_out,
    b_out,
    ln2_gain,
    ln2_bias,
    w_up,
    b_up,
    w_down,
    b_down,
    cotangent,
):
    group_rows = tokens.shape[0]
    group_size = lax.axis_size("mp")
    my_index = lax.axis_index("mp")
    row_count = group_rows // group_size
    sequences = group_rows // LEN
    heads_here = w_qkv.shape[2] // HD
    (
        gain_one,
        shift_one,
        gain_two,
        shift_two,
        bias_out,
        bias_down,
        bias_up,
        full_out,
        full_up,
        full_down,
    ) = (
        lax.all_gather(ln1_gain, "mp", axis=0, tiled=True),
        lax.all_gather(ln1_bias, "mp", axis=0, tiled=True),
        lax.all_gather(ln2_gain, "mp", axis=0, tiled=True),
        lax.all_gather(ln2_bias, "mp", axis=0, tiled=True),
        lax.all_gather(b_out, "mp", axis=0, tiled=True),
        lax.all_gather(b_down, "mp", axis=0, tiled=True),
        lax.all_gather(b_up, "mp", axis=0, tiled=True),
        lax.all_gather(w_out, "mp", axis=0, tiled=True),
        lax.all_gather(w_up, "mp", axis=1, tiled=True),
        lax.all_gather(w_down, "mp", axis=0, tiled=True),
    )
    gain_one = gain_one.astype(jnp.float32)
    shift_one = shift_one.astype(jnp.float32)
    gain_two = gain_two.astype(jnp.float32)
    shift_two = shift_two.astype(jnp.float32)
    tokens_wide = tokens.astype(jnp.float32)
    normed = layer_norm(tokens_wide, gain_one, shift_one).astype(jnp.bfloat16)
    query = (plain_dot(normed, w_qkv[0]) + b_qv[0].astype(jnp.float32)).astype(jnp.bfloat16)
    key_rows = plain_dot(normed, w_qkv[1]).astype(jnp.bfloat16)
    value_rows = (plain_dot(normed, w_qkv[2]) + b_qv[1].astype(jnp.float32)).astype(jnp.bfloat16)
    shaped = (sequences, LEN, heads_here, HD)
    query_seq = query.reshape(shaped)
    key_seq = key_rows.reshape(shaped)
    value_seq = value_rows.reshape(shaped)
    segment_seq = segment.reshape(sequences, LEN)
    attended, log_total = lax.map(attend_forward, (query_seq, key_seq, value_seq, segment_seq))
    attended = attended.reshape(group_rows, heads_here * HD)
    my_rows = lax.dynamic_slice_in_dim(tokens_wide, my_index * row_count, row_count, 0)
    attended_rows = lax.all_to_all(attended, "mp", split_axis=0, concat_axis=1, tiled=True)
    projected = plain_dot(attended_rows, full_out)
    hidden = my_rows + projected + bias_out.astype(jnp.float32)
    normed_two = layer_norm(hidden, gain_two, shift_two).astype(jnp.bfloat16)
    cot_wide = cotangent.astype(jnp.float32)
    up_proj = plain_dot(normed_two, full_up) + bias_up.astype(jnp.float32)
    active = gelu_exact(up_proj).astype(jnp.bfloat16)
    output = hidden + plain_dot(active, full_down) + bias_down.astype(jnp.float32)
    grad_up = gelu_back(up_proj, against(cotangent, full_down)).astype(jnp.bfloat16)
    grad_down = over_rows(active, cotangent)
    grad_upw = over_rows(normed_two, grad_up)
    grad_bias_up = jnp.sum(grad_up.astype(jnp.float32), axis=0)
    grad_normed_two = against(grad_up, full_up)
    grad_bias_down = jnp.sum(cot_wide, axis=0)
    grad_hidden_norm, grad_gain_two, grad_shift_two = norm_back(
        hidden, gain_two, shift_two, grad_normed_two
    )
    grad_hidden = cot_wide + grad_hidden_norm
    grad_bias_out = jnp.sum(grad_hidden, axis=0)
    grad_proj = grad_hidden.astype(jnp.bfloat16)
    grad_outw = over_rows(attended_rows, grad_proj)
    grad_attended = lax.all_to_all(
        against(grad_proj, full_out).astype(jnp.bfloat16),
        "mp",
        split_axis=1,
        concat_axis=0,
        tiled=True,
    )
    grad_query, grad_key, grad_value = lax.map(
        attend_backward,
        (query_seq, key_seq, value_seq, segment_seq, log_total, grad_attended.reshape(shaped)),
    )
    grad_query = grad_query.reshape(group_rows, heads_here * HD)
    grad_key = grad_key.reshape(group_rows, heads_here * HD)
    grad_value = grad_value.reshape(group_rows, heads_here * HD)
    grad_qkvw = jnp.stack(
        [over_rows(normed, grad_query), over_rows(normed, grad_key), over_rows(normed, grad_value)]
    )
    grad_bias_qv = jnp.stack(
        [
            jnp.sum(grad_query.astype(jnp.float32), axis=0),
            jnp.sum(grad_value.astype(jnp.float32), axis=0),
        ]
    )
    partial_normed = (
        against(grad_query, w_qkv[0]) + against(grad_key, w_qkv[1]) + against(grad_value, w_qkv[2])
    )
    grad_normed = lax.psum_scatter(
        partial_normed.astype(jnp.bfloat16), "mp", scatter_dimension=0, tiled=True
    ).astype(jnp.float32)
    grad_input_norm, grad_gain_one, grad_shift_one = norm_back(
        my_rows, gain_one, shift_one, grad_normed
    )
    grad_input = grad_hidden + grad_input_norm
    (
        share_gain_one,
        share_shift_one,
        share_gain_two,
        share_shift_two,
        share_bias_out,
        share_bias_down,
        share_bias_up,
        share_outw,
        share_upw,
        share_down,
    ) = (
        lax.psum_scatter(
            grad_gain_one.astype(jnp.bfloat16), "mp", scatter_dimension=0, tiled=True
        ).astype(jnp.float32),
        lax.psum_scatter(
            grad_shift_one.astype(jnp.bfloat16), "mp", scatter_dimension=0, tiled=True
        ).astype(jnp.float32),
        lax.psum_scatter(
            grad_gain_two.astype(jnp.bfloat16), "mp", scatter_dimension=0, tiled=True
        ).astype(jnp.float32),
        lax.psum_scatter(
            grad_shift_two.astype(jnp.bfloat16), "mp", scatter_dimension=0, tiled=True
        ).astype(jnp.float32),
        lax.psum_scatter(
            grad_bias_out.astype(jnp.bfloat16), "mp", scatter_dimension=0, tiled=True
        ).astype(jnp.float32),
        lax.psum_scatter(
            grad_bias_down.astype(jnp.bfloat16), "mp", scatter_dimension=0, tiled=True
        ).astype(jnp.float32),
        lax.psum_scatter(
            grad_bias_up.astype(jnp.bfloat16), "mp", scatter_dimension=0, tiled=True
        ).astype(jnp.float32),
        lax.psum_scatter(
            grad_outw.astype(jnp.bfloat16), "mp", scatter_dimension=0, tiled=True
        ).astype(jnp.float32),
        lax.psum_scatter(
            grad_upw.astype(jnp.bfloat16), "mp", scatter_dimension=1, tiled=True
        ).astype(jnp.float32),
        lax.psum_scatter(
            grad_down.astype(jnp.bfloat16), "mp", scatter_dimension=0, tiled=True
        ).astype(jnp.float32),
    )
    summed = lax.psum(
        (
            share_gain_one,
            share_shift_one,
            grad_qkvw,
            grad_bias_qv,
            share_outw,
            share_bias_out,
            share_gain_two,
            share_shift_two,
            share_upw,
            share_bias_up,
            share_down,
            share_bias_down,
        ),
        "dp",
    )
    return (
        output.astype(jnp.bfloat16),
        grad_input,
        summed[0],
        summed[1],
        summed[2],
        summed[3],
        summed[4],
        summed[5],
        summed[6],
        summed[7],
        summed[8],
        summed[9],
        summed[10],
        summed[11],
    )


def solution(mesh):
    placed = (
        P("dp", None),
        P("dp"),
        P("mp"),
        P("mp"),
        P(None, None, "mp"),
        P(None, "mp"),
        P("mp", None),
        P("mp"),
        P("mp"),
        P("mp"),
        P(None, "mp"),
        P("mp"),
        P("mp", None),
        P("mp"),
        P(("dp", "mp"), None),
    )
    return jax.shard_map(
        per_device,
        mesh=mesh,
        in_specs=placed,
        out_specs=(
            P(("dp", "mp"), None),
            P(("dp", "mp"), None),
            P("mp"),
            P("mp"),
            P(None, None, "mp"),
            P(None, "mp"),
            P("mp", None),
            P("mp"),
            P("mp"),
            P("mp"),
            P(None, "mp"),
            P("mp"),
            P("mp", None),
            P("mp"),
        ),
        check_vma=False,
    )
```

profile of v0, /device:TPU:0, one launch (start us, length us, event | category | flops | bytes accessed | tf_op | source)
XLA Modules:
  0.0 748.0 jit_solution(18345992957422097749)
XLA Ops:
  14.9 13.4 %all-reduce.15 = (bf16[768]{0:T(1024)(128)(2,1)S(1)}, bf16[768]{0:T(1024)(128)(2,1)S(1)}, bf16[768]{0:T(1024)(128)(2,1)S(1)}, bf16[768]{0:T(1024)(128)(2,1)S(1)}, bf16[768]{0:T(1024)(128)(2,1)S(1)}) all-reduce(bf16[768]{0:T(1024)(128)(2,1)S(1)} %dynamic-update-slice.1, ...), channel_id=1, replica_groups=mesh['dp'=8,'mp'=4] {'mp'}, use_global_device_ids=true, to_apply=%add.1 | all-reduce | flops 3840 | bytes 15360
  28.3 8.6 %copy.80 = bf16[4096,768]{0,1:T(8,128)(2,1)} copy(bf16[4096,768]{1,0:T(8,128)(2,1)} %param.19) | data formatting | bytes 12582912 | tf_op args[0]
  36.9 4.7 convert_reduce_fusion
  58.4 41.0 %while.26 = (s32[]{:T(128)}, bf16[8,512,3,64]{1,3,2,0:T(8,128)(2,1)}, f32[8,3,512]{2,1,0:T(4,128)}, bf16[8,512,3,64]{1,3,2,0:T(8,128)(2,1)}, s32[8,512]{1,0:T(8,...) while((s32[]{:T(128)}, ...), condition=%wide.region_5.6_spmd, body=%wide.region_2.5_spmd.sunk | while | flops 211909632 | bytes 11333209 | solution.py:166
  99.5 4.6 copy.84
  104.0 3.7 all_to_all.26
  110.8 3.6 all-to-all-start
  115.2 9.2 %convert_element_type.163 = f32[4096,768]{0,1:T(8,128)} convert(bf16[4096,768]{0,1:T(8,128)(2,1)} %copy.80) | non-fusion elementwise | flops 3145728 | bytes 18874368 | tf_op jit(solution)/shard_map/convert_element_type | solution.py:156
  124.4 16.9 %all-gather = bf16[4,1,768]{2,1,0:T(2,128)(2,1)S(1)} all-gather(bf16[1,1,768]{2,1,0:T(2,128)(2,1)S(1)} %reshape.310), channel_id=1, replica_groups=mesh['dp'=8,'mp'=4] {'mp'}, dimensions={0}, use_global_device_ids=true | all-gather | bytes 7680 | tf_op jit(solution)/shard_map/all_gather | solution.py:147
  144.1 4.3 fusion.91
  148.8 37.7 %multiply_convert_fusion.1 = (bf16[1024,3072]{1,0:T(8,128)(2,1)}, f32[1024,3072]{1,0:T(8,128)}, f32[1024,3072]{1,0:T(8,128)}) fusion(f32[3072]{0:T(1024)S(1)} %bitcast.224, bf16[768,3072]{1,0:T(8,128)(2,1)} %all-gather.7.cloned.1.call-done, f32[1024,768]{0,1:T(8,128)S(1)} %get-tuple-element.289, f32[768]{0:T(1024)S(1)} %convert_element_type.172, ...), kind=kOutput, calls=%fused_computation.70 | convolution fusion | flops 5043388416 | bytes 39348224 | tf_op jit(solution)/shard_map/dot_general | solution.py:31
  186.5 18.5 %fusion.93 = (bf16[3072]{0:T(1024)(128)(2,1)S(1)}, bf16[1024,3072]{1,0:T(8,128)(2,1)}) fusion(f32[1024,3072]{1,0:T(8,128)} %get-tuple-element.275, bf16[1024,768]{1,0:T(8,128)(2,1)} %param.33, bf16[3072,768]{1,0:T(8,128)(2,1)} %all-gather.9.cloned.1.call-done, f32[1024,3072]{1,0:T(8,128)} %get-tuple-element.290, f32[3072]{0:T(1024)S(1)} %bitcast.225), kind=kOutput, calls=%fused_computation.165 | convolution fusion | flops 4882166784 | bytes 37767168 | tf_op jit(solution)/shard_map/dot_general | solution.py:41
  205.0 9.8 %fusion.92 = (bf16[768]{0:T(1024)(128)(2,1)S(1)}, f32[1024,768]{1,0:T(8,128)}) fusion(bf16[1024,3072]{1,0:T(8,128)(2,1)} %get-tuple-element.294, bf16[768,3072]{1,0:T(8,128)(2,1)} %all-gather.7.cloned.1.call-done), kind=kOutput, calls=%fused_computation.164 | convolution fusion | flops 4832623616 | bytes 14157312 | tf_op jit(solution)/shard_map/dot_general | solution.py:41
  214.8 3.6 copy.88
  227.5 10.1 %convolution_convert_fusion.1 = bf16[768,3072]{1,0:T(8,128)(2,1)} fusion(bf16[1024,3072]{1,0:T(8,128)(2,1)} %get-tuple-element.294, f32[1024,768]{0,1:T(8,128)S(1)} %get-tuple-element.289, f32[768]{0:T(1024)S(1)} %convert_element_type.172, f32[768]{0:T(1024)S(1)} %convert_element_type.171, f32[1024]{0:T(1024)S(1)} %fusion.85, ...), kind=kOutput, calls=%fused_computation.88 | convolution fusion | flops 4838129664 | bytes 14170112 | tf_op jit(solution)/shard_map/dot_general | solution.py:35
  237.7 4.3 convolution_convert_fusion.3
  242.0 4.4 all-to-all-start.1
  246.4 9.1 %convolution_convert_fusion = bf16[3072,768]{1,0:T(8,128)(2,1)} fusion(bf16[1024,3072]{1,0:T(8,128)(2,1)} %get-tuple-element.274, bf16[1024,768]{1,0:T(8,128)(2,1)} %param.33), kind=kOutput, calls=%fused_computation.87 | convolution fusion | flops 4834197504 | bytes 12582912 | tf_op jit(solution)/shard_map/dot_general | solution.py:35
  255.6 14.0 %all-to-all-done.1 = bf16[1024,4,192]{0,2,1:T(8,128)(2,1)} async-done(((bf16[1024,4,192]{0,2,1:T(8,128)(2,1)}), bf16[1024,4,192]{0,2,1:T(8,128)(2,1)}, u32[]{:S(2)}, u32[]{:S(2)}) %all-to-all-start.1) | async-done | bytes 1572896 | tf_op jit(solution)/shard_map/all_to_all | solution.py:190
  269.6 3.9 copy.89
  284.3 102.6 %while.27 = (s32[]{:T(128)}, bf16[8,512,3,64]{1,3,2,0:T(8,128)(2,1)}, bf16[8,512,3,64]{1,3,2,0:T(8,128)(2,1)}, bf16[8,512,3,64]{1,3,2,0:T(8,128)(2,1)}, bf16[8,5...) while((s32[]{:T(128)}, ...), condition=%wide.region_12.13_spmd, body=%wide.region_10.12_spmd.sunk | while | flops 511933440 | bytes 26126452 | solution.py:197
  393.6 6.4 fusion.71
  400.0 6.3 fusion.74
  406.3 12.1 %add_convert_fusion = bf16[4096,768]{0,1:T(8,128)(2,1)} fusion(f32[4096,768]{0,1:T(8,128)} %fusion.74, f32[4096,768]{0,1:T(8,128)} %fusion.71, bf16[4096,192]{0,1:T(8,128)(2,1)S(1)} %bitcast.206, bf16[3,768,192]{1,2,0:T(8,128)(2,1)S(1)} %copy-done.24), kind=kOutput, calls=%fused_computation.68 | convolution fusion | flops 1217396736 | bytes 33325056 | tf_op jit(solution)/shard_map/dot_general | solution.py:41
  427.1 6.8 convolution_bitcast_fusion
  434.0 5.2 convolution_bitcast_fusion.1
  442.9 33.5 %reduce-scatter.5.cloned.1.call-done = bf16[1024,768]{0,1:T(8,128)(2,1)} async-done(((bf16[4096,768]{0,1:T(8,128)(2,1)}), bf16[1024,768]{0,1:T(8,128)(2,1)}) %reduce-scatter.5.cloned.1.call-update) | async-done | bytes 1572880 | tf_op jit(solution)/shard_map/reduce_scatter | solution.py:216
  479.6 3.6 fusion.67
  483.3 5.3 add_add_fusion.2
  490.3 11.3 %all-reduce.14 = (bf16[768]{0:T(1024)(128)(2,1)S(1)}, bf16[768]{0:T(1024)(128)(2,1)S(1)}, bf16[768]{0:T(1024)(128)(2,1)S(1)}, bf16[768]{0:T(1024)(128)(2,1)S(1)}...) all-reduce(bf16[768]{0:T(1024)(128)(2,1)S(1)} %dynamic-update-slice, ...), channel_id=1, replica_groups=mesh['dp'=8,'mp'=4] {'mp'}, use_global_device_ids=true, to_apply=%add.5 | all-reduce | flops 8448 | bytes 33792
  501.6 9.5 %add_convert_fusion.3 = bf16[1024,768]{0,1:T(8,128)(2,1)} fusion(f32[1024,768]{0,1:T(8,128)S(1)} %get-tuple-element.289, bf16[1024,3072]{1,0:T(8,128)(2,1)} %get-tuple-element.274, bf16[3072,768]{1,0:T(8,128)(2,1)} %all-gather.9.cloned.1.call-done, f32[768]{0:T(1024)S(1)} %convert_element_type.176), kind=kOutput, calls=%fused_computation.109 | convolution fusion | flops 4834197504 | bytes 15731712 | tf_op jit(solution)/shard_map/dot_general | solution.py:31
  516.5 221.4 %all-reduce.20 = (f32[192]{0:T(256)}, f32[192]{0:T(256)}, f32[2,192]{1,0:T(2,128)}, f32[192,768]{1,0:T(8,128)}, f32[192]{0:T(256)}, /*index=5*/f32[192]{0:T(256)...) all-reduce(f32[192]{0:T(256)S(1)} %get-tuple-element.302, ...), channel_id=1, replica_groups=mesh['dp'=8,'mp'=4] {'dp'}, use_global_device_ids=true, to_apply=%region_20.21 | all-reduce | flops 1329408 | bytes 7981056 | tf_op jit(solution)/shard_map/psum | solution.py:266
  (295 shorter events, 224.1 us)
Async XLA Ops:
  7.2 135.8 %all-gather.5.cloned.1.call-start = ((), (), s32[]{:S(2)}) async-start(), calls=%async_computation.6 | async-start | bytes 1474560 | tf_op jit(solution)/shard_map/all_gather | solution.py:148
  7.9 140.9 %all-gather.7.cloned.1.call-start = ((), (), s32[]{:S(2)}) async-start(), calls=%async_computation.7 | async-start | bytes 5898240 | tf_op jit(solution)/shard_map/all_gather | solution.py:149
  28.3 16.4 %copy-start.26 = (f32[768]{0:T(1024)}, f32[768]{0:T(1024)S(1)}, u32[]{:S(2)}) copy-start(f32[768]{0:T(1024)S(1)} %convert_element_type.164) | copy-start | bytes 9220
  36.9 6.0 copy-start
  44.7 3.5 copy-start.23
  48.2 5.1 copy-start.19
  99.4 8.3 %copy-start.9 = (bf16[8,512,3,64]{1,3,2,0:T(8,128)(2,1)}, bf16[8,512,3,64]{1,3,2,0:T(8,128)(2,1)S(1)}, u32[]{:S(2)}) copy-start(bf16[8,512,3,64]{1,3,2,0:T(8,128)(2,1)S(1)} %get-tuple-element.505) | copy-start | bytes 4718596
  99.5 8.3 %copy-start.10 = (bf16[8,512,3,64]{1,3,2,0:T(8,128)(2,1)}, bf16[8,512,3,64]{1,3,2,0:T(8,128)(2,1)S(1)}, u32[]{:S(2)}) copy-start(bf16[8,512,3,64]{1,3,2,0:T(8,128)(2,1)S(1)} %get-tuple-element.506) | copy-start | bytes 4718596
  99.5 8.3 %copy-start.28 = (s32[8,512]{1,0:T(8,128)}, s32[8,512]{1,0:T(8,128)S(1)}, u32[]{:S(2)}) copy-start(s32[8,512]{1,0:T(8,128)S(1)} %get-tuple-element.531) | copy-start | bytes 49156
  110.8 32.2 %all-to-all-start = ((bf16[4,1024,192]{1,2,0:T(8,128)(2,1)}), bf16[4,1024,192]{1,2,0:T(8,128)(2,1)S(1)}, u32[]{:S(2)}, u32[]{:S(2)}) async-start(bf16[4,1024,192]{1,2,0:T(8,128)(2,1)} %copy.85), calls=%async_computation | async-start | bytes 3145728 | tf_op jit(solution)/shard_map/all_to_all | solution.py:169
  114.4 72.2 %all-gather.9.cloned.1.call-start = ((), (), s32[]{:S(2)}) async-start(), calls=%async_computation.8 | async-start | bytes 5898240 | tf_op jit(solution)/shard_map/all_gather | solution.py:150
  115.1 9.3 %copy-start.31 = (bf16[768]{0:T(1024)(128)(2,1)S(1)}, bf16[768]{0:T(1024)(128)(2,1)}, u32[]{:S(2)}) copy-start(bf16[768]{0:T(1024)(128)(2,1)} %param.30) | copy-start | bytes 4612
  115.1 26.2 %copy-start.17 = (bf16[1024,768]{1,0:T(8,128)(2,1)S(1)}, bf16[1024,768]{1,0:T(8,128)(2,1)}, u32[]{:S(2)}) copy-start(bf16[1024,768]{1,0:T(8,128)(2,1)} %param.33) | copy-start | bytes 4718596
  115.1 327.7 %reduce-scatter.7.cloned.1.call-start = ((), (), s32[]{:S(2)}) async-start(), calls=%async_computation.11 | async-start | bytes 1474560 | tf_op jit(solution)/shard_map/reduce_scatter | solution.py:256
  227.4 215.4 %reduce-scatter.9.cloned.1.call-start = ((), (), s32[]{:S(2)}) async-start(), calls=%async_computation.12 | async-start | bytes 5898240 | tf_op jit(solution)/shard_map/reduce_scatter | solution.py:259
  242.0 27.7 %all-to-all-start.1 = ((bf16[1024,4,192]{0,2,1:T(8,128)(2,1)}), bf16[1024,4,192]{0,2,1:T(8,128)(2,1)}, u32[]{:S(2)}, u32[]{:S(2)}) async-start(bf16[1024,4,192]{0,2,1:T(8,128)(2,1)} %bitcast.218), calls=%async_computation.1 | async-start | bytes 3145728 | tf_op jit(solution)/shard_map/all_to_all | solution.py:190
  246.4 196.5 %reduce-scatter.11.cloned.1.call-start = ((), (), s32[]{:S(2)}) async-start(), calls=%async_computation.13 | async-start | bytes 5898240 | tf_op jit(solution)/shard_map/reduce_scatter | solution.py:262
  255.6 220.8 %reduce-scatter.5.cloned.1.call-start = ((), (), s32[]{:S(2)}) async-start(), calls=%async_computation.9 | async-start | bytes 7864320 | tf_op jit(solution)/shard_map/reduce_scatter | solution.py:216
  386.9 3.1 copy-start.18
  390.0 16.3 %copy-start.16 = (bf16[24,8,8,512]{3,1,2,0:T(8,128)(2,1)}, bf16[24,8,8,512]{3,1,2,0:T(8,128)(2,1)S(1)}, u32[]{:S(2)}) copy-start(bf16[24,8,8,512]{3,1,2,0:T(8,128)(2,1)S(1)} %copy.116) | copy-start | bytes 4718596
  393.6 6.5 copy-start.14
  418.5 3.1 copy-start.32
  418.5 319.5 %all-reduce.19.cloned.1.call-start = ((), (), s32[]{:S(2)}) async-start(), calls=%async_computation.10 | async-start | bytes 3538944 | tf_op jit(solution)/shard_map/psum | solution.py:266
  422.0 3.0 copy-start.8
  427.1 6.9 copy-start.13
  427.1 12.0 %slice-start = ((s8[6291456]{0:T(1024)(128)(4,1)}), s8[4194304]{0:T(1024)(128)(4,1)S(1)}, s32[]{:S(2)}) async-start(s8[6291456]{0:T(1024)(128)(4,1)} %bitcast.214), calls=%async_computation.14 | async-start | bytes 8388608
  434.0 5.2 copy-start.15
  434.0 5.2 slice-start.1
  441.4 34.9 %copy-start.27 = (f32[768]{0:T(1024)S(1)}, f32[768]{0:T(1024)}, u32[]{:S(2)}) copy-start(f32[768]{0:T(1024)} %copy-done.26) | copy-start | bytes 9220
  476.3 3.3 copy-start.4
  479.6 3.7 copy-start.3
  479.6 3.7 copy-start.6
  (13 other events, 24.4 us)
Sparse Core Ops, SparseCore 0:
  9.5 20.3 all-gather.4
  31.5 37.4 all-gather.6
  116.7 44.5 all-gather.8
  227.6 29.4 reduce-scatter.6
  259.4 47.5 reduce-scatter.8
  309.4 47.9 reduce-scatter.10
  418.6 57.6 reduce-scatter.4
  480.5 119.6 all-reduce.18
where the time goes:
time: 760 us; the launch traced here: 748 us
  blocking collectives  263 us (35%)
  matrix products  259 us (34%)
  local copies, waits for them, and re-layouts  77.2 us (10%)
  other arithmetic  73.1 us (10%)
  waiting for transfers between devices  49.7 us (7%)
  between operations  17.2 us (2%)
  starting transfers between devices  8.28 us (1%)
    psum x1, blocking collectives, per_device(): lax.psum((share_gain_one, share_shift_one, grad_qkvw, grad_bias_qv, share...  221 us
    dot_general x6, matrix products, against(): lax.dot_general(left, right, (((1,), (1,)), ((), ())), preferred_element_...  57.4 us
    dot_general x6, matrix products, plain_dot(): return jnp.dot(left, right, preferred_element_type=jnp.float32)  55.7 us
    dot_general x6, matrix products, over_rows(): lax.dot_general(left, right, (((0,), (0,)), ((), ())), preferred_element_...  36 us
    unnamed x95, local copies, waits for them, and re-layouts  33.7 us
    reduce_scatter x1, waiting for transfers between devices, per_device(): lax.psum_scatter(partial_normed.astype(jnp.bfloat16), 'mp', scatter_dimen...  33.5 us
    unnamed x2, blocking collectives  24.7 us
    dot_general x16, matrix products, head_scores(): jnp.einsum('qhd,khd->hqk', query_heads, key_heads, preferred_element_type...  23.6 us
  transfers between devices with their start and end apart: 10, of which 2 were waited for; matrix products, arithmetic and copies ran while one was open for 48% of the time, Pallas kernels for 0%

commit v1 on v0

v1 whole, which is shorter than its diff:
```python
import jax
import jax.numpy as jnp
from jax import lax
from jax.experimental import pallas as pl
from jax.experimental.pallas import tpu as pltpu
from jax.sharding import PartitionSpec as P

HD = 64
LEN = 512
F32 = jnp.float32
BF16 = jnp.bfloat16
VMEM_LIMIT = 64 * 1024 * 1024 - 128 * 1024


def nn(left, right):
    return jnp.dot(left, right, preferred_element_type=F32)


def nt(left, right):
    return lax.dot_general(left, right, (((1,), (1,)), ((), ())), preferred_element_type=F32)


def tn(left, right):
    return lax.dot_general(left, right, (((0,), (0,)), ((), ())), preferred_element_type=F32)


def rows_of(index, count):
    return pl.ds(pl.multiple_of(index * count, count), count)


def normal_of(values):
    centered = values - jnp.mean(values, axis=-1, keepdims=True)
    spread = jnp.mean(centered * centered, axis=-1, keepdims=True)
    inverse = lax.rsqrt(spread + 1e-06)
    return centered * inverse, inverse


def norm_input_back(normal, inverse, scaled):
    inner = jnp.mean(scaled * normal, axis=-1, keepdims=True)
    return inverse * (scaled - jnp.mean(scaled, axis=-1, keepdims=True) - normal * inner)


def column_sum(values):
    return jnp.sum(values, axis=0, keepdims=True)


def each(count, body):
    lax.fori_loop(0, count, lambda i, carry: (body(i), carry)[1], 0)


def mask_bias(bias, seg_col, seg_row, sequence):
    rows = rows_of(sequence, LEN)
    one = seg_col[rows, :]
    other = seg_row[pl.ds(sequence, 1), :]
    row_ids = lax.broadcasted_iota(jnp.int32, (LEN, LEN), 0)
    col_ids = lax.broadcasted_iota(jnp.int32, (LEN, LEN), 1)
    allowed = ((one == other) & (other != 0)) | (row_ids == col_ids)
    bias[...] = jnp.where(allowed, 0.0, -1e30)


def forward_kernel(
    x, seg_col, seg_row, wqkv, w_out, g1, b1, bqv, b_out, g2, b2,
    normed, qs, ks, vs, stats, attended, hidden, n2, bias,
):
    count = x.shape[0]
    tile = 256
    sequences = count // LEN
    pairs = x.shape[1] // 128

    def ln_one(i):
        r = rows_of(i, tile)
        normal, _ = normal_of(x[r, :].astype(F32))
        normed[r, :] = (normal * g1[...] + b1[...]).astype(BF16)

    each(count // tile, ln_one)

    def project(i):
        r = rows_of(i, LEN)
        value = normed[r, :]
        qs[r, :] = ((nt(value, wqkv[0]) + bqv[0:1, :]).astype(BF16).astype(F32) * (HD**-0.5)).astype(BF16)
        ks[r, :] = nt(value, wqkv[1]).astype(BF16)
        vs[r, :] = (nt(value, wqkv[2]) + bqv[1:2, :]).astype(BF16)

    each(count // LEN, project)
    lane = lax.broadcasted_iota(jnp.int32, (LEN, 128), 1)
    first = lane < HD

    def sequence_step(s):
        mask_bias(bias, seg_col, seg_row, s)
        r = rows_of(s, LEN)
        stats[r, :] = jnp.zeros((LEN, 128), F32)

        def pair_step(p):
            c = rows_of(p, 128)
            q2, k2, v2 = qs[r, c], ks[r, c], vs[r, c]
            results = []
            kept = stats[r, :]
            for half in range(2):
                mine = first if half == 0 else ~first
                scores = nt(jnp.where(mine, q2, jnp.zeros_like(q2)), k2) + bias[...]
                top = jnp.max(scores, axis=-1, keepdims=True)
                expo = jnp.exp(scores - top)
                total = jnp.sum(expo, axis=-1, keepdims=True)
                results.append(nn(expo.astype(BF16), v2) * (1.0 / total))
                kept = jnp.where(lane == 2 * p + half, top + jnp.log(total), kept)
            stats[r, :] = kept
            attended[r, c] = jnp.where(first, results[0], results[1]).astype(BF16)

        each(pairs, pair_step)

    each(sequences, sequence_step)

    def out_step(i):
        r = rows_of(i, tile)
        value = x[r, :].astype(F32) + nn(attended[r, :], w_out[...]) + b_out[...]
        hidden[r, :] = value
        normal, _ = normal_of(value)
        n2[r, :] = (normal * g2[...] + b2[...]).astype(BF16)

    each(count // tile, out_step)


def feed_kernel(
    n2, cot, w_up, w_down, b_up, b_down, hidden, attended, w_out, g2,
    out, grad_hidden, grad_att, gw_down, gw_up, gw_out, vec,
    act, gup,
):
    count, width = n2.shape
    groups = w_up.shape[0]
    piece = 256
    per_group = w_up.shape[2] // piece
    vec[...] = jnp.zeros_like(vec)

    def chunk(j):
        m, part = j // per_group, j % per_group
        c = rows_of(part, piece)
        whole = rows_of(j, piece)
        wu, wd = w_up[m, :, c], w_down[m, c, :]
        bias = b_up[pl.ds(m, 1), c]

        def rows_step(i):
            r = rows_of(i, LEN)
            up = nn(n2[r, :], wu) + bias
            half_cdf = 0.5 * (1.0 + lax.erf(up * (0.5**0.5)))
            slope = half_cdf + up * (jnp.exp(-0.5 * up * up) * 0.3989422804014327)
            act[r, whole] = (up * half_cdf).astype(BF16)
            grad = (nt(cot[r, :], wd) * slope).astype(BF16)
            gup[r, whole] = grad
            vec[pl.ds(8 + m, 1), c] += column_sum(grad.astype(F32))

        each(count // LEN, rows_step)
        gw_down[m, c, :] = tn(act[:, whole], cot[...]).astype(BF16)
        gw_up[m, :, c] = tn(n2[...], gup[:, whole]).astype(BF16)

    each(groups * per_group, chunk)
    tile = 256

    def rows_step(i):
        r = rows_of(i, tile)
        incoming = jnp.zeros((tile, width), F32)
        result = hidden[r, :] + b_down[...]
        for m in range(groups):
            c = pl.ds(m * width, width)
            incoming += nt(gup[r, c], w_up[m])
            result += nn(act[r, c], w_down[m])
        out[r, :] = result.astype(BF16)
        normal, inverse = normal_of(hidden[r, :])
        wide = cot[r, :].astype(F32)
        grad = wide + norm_input_back(normal, inverse, incoming * g2[...])
        grad_hidden[r, :] = grad
        vec[4:5, :] += column_sum(grad)
        vec[5:6, :] += column_sum(incoming * normal)
        vec[6:7, :] += column_sum(incoming)
        vec[7:8, :] += column_sum(wide)
        grad_att[r, :] = nt(grad.astype(BF16), w_out[...]).astype(BF16)

    each(count // tile, rows_step)
    gw_out[...] = tn(attended[...], grad_hidden[...].astype(BF16)).astype(BF16)


def backward_kernel(
    x, seg_col, seg_row, normed, qs, ks, vs, stats, grad_att, grad_hidden, wqkv, g1,
    grad_x, gw_qkv, vec, bias, stat_rows, dq, dk, dv,
):
    count, width = x.shape
    sequences = count // LEN
    pairs = width // 128
    vec[...] = jnp.zeros_like(vec)
    lane = lax.broadcasted_iota(jnp.int32, (LEN, 128), 1)
    first = lane < HD

    def sequence_step(s):
        mask_bias(bias, seg_col, seg_row, s)
        r = rows_of(s, LEN)
        stat_rows[...] = stats[r, :].T

        def pair_step(p):
            c = rows_of(p, 128)
            q2, k2, v2, d2 = qs[r, c], ks[r, c], vs[r, c], grad_att[r, c]
            rq, rk, rv = 0.0, 0.0, 0.0
            for half in range(2):
                mine = first if half == 0 else ~first
                qm = jnp.where(mine, q2, jnp.zeros_like(q2))
                km = jnp.where(mine, k2, jnp.zeros_like(k2))
                dm = jnp.where(mine, d2, jnp.zeros_like(d2))
                probs = jnp.exp(nt(k2, qm) + bias[...] - stat_rows[pl.ds(2 * p + half, 1), :])
                grad_probs = nt(v2, dm)
                inner = jnp.sum(probs * grad_probs, axis=0, keepdims=True)
                grad_scores = (probs * (grad_probs - inner)).astype(BF16)
                rv += nn(probs.astype(BF16), dm)
                rk += nn(grad_scores, qm)
                rq += tn(grad_scores, km)
            dq[r, c] = (rq * (HD**-0.5)).astype(BF16)
            dk[r, c] = rk.astype(BF16)
            dv[r, c] = rv.astype(BF16)

        each(pairs, pair_step)

    each(sequences, sequence_step)
    for k, grad in enumerate((dq, dk, dv)):

        def weight_step(j, k=k, grad=grad):
            c = rows_of(j, 256)
            gw_qkv[k, c, :] = tn(grad[:, c], normed[...]).astype(BF16)

        each(width // 256, weight_step)
    tile = 256

    def rows_step(i):
        r = rows_of(i, tile)
        q, k, v = dq[r, :], dk[r, :], dv[r, :]
        incoming = nn(q, wqkv[0]) + nn(k, wqkv[1]) + nn(v, wqkv[2])
        normal, inverse = normal_of(x[r, :].astype(F32))
        grad_x[r, :] = grad_hidden[r, :] + norm_input_back(normal, inverse, incoming * g1[...])
        vec[0:1, :] += column_sum(incoming * normal)
        vec[1:2, :] += column_sum(incoming)
        vec[2:3, :] += column_sum(q.astype(F32))
        vec[3:4, :] += column_sum(v.astype(F32))

    each(count // tile, rows_step)


def local_call(kernel, outs, scratch, *args):
    spec = pl.BlockSpec(memory_space=pltpu.VMEM)
    return pl.pallas_call(
        kernel,
        out_shape=outs,
        in_specs=[spec] * len(args),
        out_specs=[spec] * len(outs),
        scratch_shapes=scratch,
        compiler_params=pltpu.CompilerParams(vmem_limit_bytes=VMEM_LIMIT),
    )(*args)


def gathered(value):
    return lax.all_gather(value, "mp", axis=0)


def per_device(
    tokens, segment, ln1_gain, ln1_bias, w_qkv, b_qv, w_out, b_out, ln2_gain, ln2_bias, w_up, b_up, w_down, b_down,
    cotangent,
):
    mp = lax.axis_size("mp")
    me = lax.axis_index("mp")
    width = tokens.shape[1]
    count = tokens.shape[0] // mp
    part = width // mp
    feed = w_up.shape[1]
    x = lax.dynamic_slice_in_dim(tokens, me * count, count, 0)
    seg = lax.dynamic_slice_in_dim(segment, me * count, count, 0)
    seg_col = seg.reshape(count, 1)
    seg_row = seg.reshape(count // LEN, LEN)
    small = jnp.concatenate([ln1_gain, ln1_bias, b_qv[0], b_qv[1], b_out, ln2_gain, ln2_bias, b_down, b_up])
    small = gathered(small.reshape(1, -1)).reshape(mp, -1)
    vectors = small[:, : 8 * part].reshape(mp, 8, part).transpose(1, 0, 2).reshape(8, width).astype(F32)
    b_up_full = small[:, 8 * part :].astype(F32)
    wqkv = gathered(w_qkv.swapaxes(1, 2)).transpose(1, 0, 2, 3).reshape(3, width, width)
    full_out = gathered(w_out).reshape(width, width)
    full_up = gathered(w_up)
    full_down = gathered(w_down)
    g1, b1, bqv, bo, g2, b2, bd = (
        vectors[0:1], vectors[1:2], vectors[2:4], vectors[4:5], vectors[5:6], vectors[6:7], vectors[7:8],
    )
    wide = jax.ShapeDtypeStruct((count, width), F32)
    narrow = jax.ShapeDtypeStruct((count, width), BF16)
    weight = jax.ShapeDtypeStruct((mp, feed, width), BF16)
    mask = pltpu.VMEM((LEN, LEN), F32)
    normed, qs, ks, vs, stats, attended, hidden, n2 = local_call(
        forward_kernel,
        [narrow] * 4 + [jax.ShapeDtypeStruct((count, 128), F32), narrow, wide, narrow],
        [mask],
        x, seg_col, seg_row, wqkv, full_out, g1, b1, bqv, bo, g2, b2,
    )
    output, grad_hidden, grad_att, gw_down, gw_up, gw_out, vec_a = local_call(
        feed_kernel,
        [narrow, wide, narrow, weight, weight, jax.ShapeDtypeStruct((width, width), BF16),
         jax.ShapeDtypeStruct((16, width), F32)],
        [pltpu.VMEM((count, mp * feed), BF16), pltpu.VMEM((count, mp * feed), BF16)],
        n2, cotangent, full_up, full_down, b_up_full, bd, hidden, attended, full_out, g2,
    )
    grad_x, gw_qkv, vec_b = local_call(
        backward_kernel,
        [wide, jax.ShapeDtypeStruct((3, width, width), BF16), jax.ShapeDtypeStruct((16, width), F32)],
        [mask, pltpu.VMEM((128, LEN), F32)] + [pltpu.VMEM((count, width), BF16)] * 3,
        x, seg_col, seg_row, normed, qs, ks, vs, stats, grad_att, grad_hidden, wqkv, g1,
    )
    packed = jnp.concatenate(
        [gw_down, gw_up, gw_out.reshape(mp, part, width),
         gw_qkv.reshape(3, mp, part, width).transpose(1, 0, 2, 3).reshape(mp, 3 * part, width)],
        axis=1,
    )
    share = lax.psum_scatter(packed, "mp", scatter_dimension=0, tiled=False)
    share = lax.psum(share, "dp").astype(F32)
    vec = lax.psum(vec_a + vec_b, ("dp", "mp"))
    eight = lax.dynamic_slice_in_dim(vec[:8], me * part, part, 1)
    grad_b_up = lax.dynamic_slice_in_dim(vec[8 : 8 + mp], me, 1, 0).reshape(-1)
    two = 2 * feed
    g_qkv = share[two + part :].reshape(3, part, width).swapaxes(1, 2)
    return (
        output, grad_x, eight[0], eight[1], g_qkv, eight[2:4], share[two : two + part], eight[4], eight[5], eight[6],
        share[feed:two], grad_b_up, share[:feed], eight[7],
    )


def solution(mesh):
    rows = P(("dp", "mp"), None)
    return jax.shard_map(
        per_device,
        mesh=mesh,
        in_specs=(
            P("dp", None), P("dp"), P("mp"), P("mp"), P(None, None, "mp"), P(None, "mp"), P("mp", None), P("mp"),
            P("mp"), P("mp"), P(None, "mp"), P("mp"), P("mp", None), P("mp"), rows,
        ),
        out_specs=(
            rows, rows, P("mp"), P("mp"), P(None, None, "mp"), P(None, "mp"), P("mp", None), P("mp"), P("mp"), P("mp"),
            P(None, "mp"), P("mp"), P("mp", None), P("mp"),
        ),
        check_vma=False,
    )
```

time: 760 us -> 519 us (0.68); the launches traced: 748 us -> 519 us
  matrix products: 259 us -> 0 us
  waiting for transfers between devices: 49.7 us -> 291 us
  blocking collectives: 263 us -> 49.5 us
  Pallas kernels: 0 us -> 128 us
  other arithmetic: 73.1 us -> 9.56 us
  local copies, waits for them, and re-layouts: 77.2 us -> 26.2 us
  starting transfers between devices: 8.28 us -> 0.23 us
    dot_general x74 -> x0, matrix products: 259 us -> none  [the longest x6 57.4 us: against(): lax.dot_general(left, right, (((1,), (1,)), ((), ())), preferred_element_...]
    psum x1, blocking collectives: 221 us -> 43.2 us  [per_device(): vec = lax.psum(vec_a + vec_b, ('dp', 'mp'))]
    pallas_call x0 -> x3, Pallas kernels: none -> 128 us  [local_call(): pl.pallas_call(kernel, out_shape=outs, in_specs=[spec] * len(args), out_s...]
    psum x1, waiting for transfers between devices: 0.01 us -> 98 us  [per_device(): share = lax.psum(share, 'dp').astype(F32)]
    all_gather x3 -> x4, waiting for transfers between devices: 0.02 us -> 79.8 us  [gathered(): return lax.all_gather(value, 'mp', axis=0)]
    reduce_scatter x4 -> x1, waiting for transfers between devices: 33.5 us -> 111 us  [per_device(): share = lax.psum_scatter(packed, 'mp', scatter_dimension=0, tiled=False)]
    unnamed x95 -> x28, local copies, waits for them, and re-layouts: 33.7 us -> 1.43 us
    reduce_sum x19 -> x0, other arithmetic: 30.8 us -> none  [the longest x3 8.23 us: layer_norm(): return centered * lax.rsqrt(spread + 1e-06) * norm_gain + norm_shift]
  transfers between devices with their start and end apart: 10 -> 6, of which waited for: 2 -> 6; matrix products, arithmetic and copies ran while one was open for 48% -> 3% of each run, Pallas kernels for 0% -> 6%
where the time goes in v1:
time: 519 us
  waiting for transfers between devices  291 us (56%)
  Pallas kernels  128 us (25%)
  blocking collectives  49.5 us (10%)
  local copies, waits for them, and re-layouts  26.2 us (5%)
  between operations  14.4 us (3%)
  other arithmetic  9.56 us (2%)
    pallas_call x3, Pallas kernels, local_call(): pl.pallas_call(kernel, out_shape=outs, in_specs=[spec] * len(args), out_s...  128 us
    reduce_scatter x1, waiting for transfers between devices, per_device(): share = lax.psum_scatter(packed, 'mp', scatter_dimension=0, tiled=False)  111 us
    psum x1, waiting for transfers between devices, per_device(): share = lax.psum(share, 'dp').astype(F32)  98 us
    all_gather x4, waiting for transfers between devices, gathered(): return lax.all_gather(value, 'mp', axis=0)  79.8 us
    psum x1, blocking collectives, per_device(): vec = lax.psum(vec_a + vec_b, ('dp', 'mp'))  43.2 us
  transfers between devices with their start and end apart: 6, of which 6 were waited for; matrix products, arithmetic and copies ran while one was open for 3% of the time, Pallas kernels for 6%

profile of v1, /device:TPU:0, one launch (start us, length us, event | category | flops | bytes accessed | tf_op | source)
XLA Modules:
  0.0 518.5 jit_solution(13830090980131008169)
XLA Ops:
  7.3 0.7 all-gather.11.cloned.1.call-update
  8.0 0.7 all-gather.13.cloned.1.call-update
  8.8 0.7 all-gather.15.cloned.1.call-update
  10.1 0.7 dynamic_slice.13
  11.4 1.0 copy.44.seg_col
  12.6 6.2 %all-gather.5 = bf16[4,1,2304]{2,1,0:T(2,128)(2,1)S(1)} all-gather(bf16[1,1,2304]{2,1,0:T(2,128)(2,1)S(1)} %reshape.88), channel_id=4, replica_groups=mesh['dp'=8,'mp'=4] {'mp'}, dimensions={0}, use_global_device_ids=true | all-gather | bytes 23040 | tf_op jit(solution)/shard_map/all_gather | solution.py:256
  19.0 0.7 slice.105.g2
  19.7 0.7 slice.97.g1
  20.4 0.7 slice.103.b_out
  21.0 0.7 slice.107.b2
  21.7 0.7 slice.99.b1
  22.4 0.7 slice.101.bqv
  23.1 0.7 slice.110.b_down
  23.7 2.7 constant_dynamic-slice_fusion.1.x
  27.0 16.2 %all-gather.11.cloned.1.call-done = bf16[12,192,768]{2,1,0:T(8,128)(2,1)} async-done(((bf16[3,192,768]{2,1,0:T(8,128)(2,1)}), bf16[12,192,768]{2,1,0:T(8,128)(2,1)}) %all-gather.11.cloned.1.call-update) | async-done | bytes 3538960 | tf_op jit(solution)/shard_map/all_gather | solution.py:256
  43.1 4.0 copy.42
  47.2 15.0 %all-gather.13.cloned.1.call-done.w_out = bf16[768,768]{1,0:T(8,128)(2,1)} async-done(((bf16[192,768]{1,0:T(8,128)(2,1)}), bf16[768,768]{1,0:T(8,128)(2,1)}) %all-gather.13.cloned.1.call-update) | async-done | bytes 1179664 | tf_op jit(solution)/shard_map/all_gather | solution.py:256
  62.2 29.3 %shard_map.254 = (bf16[1024,768]{1,0:T(8,128)(2,1)}, bf16[1024,768]{1,0:T(8,128)(2,1)}, bf16[1024,768]{1,0:T(8,128)(2,1)}, bf16[1024,768]{1,0:T(8,128)(2,1)}, f3...) custom-call(bf16[1024,768]{1,0:T(8,128)(2,1)} %constant_dynamic-slice_fusion.1.x, ...), custom_call_target="tpu_custom_call" | custom-call | tf_op jit(solution)/shard_map/pallas_call | solution.py:245
  91.5 9.7 %all-gather.15.cloned.1.call-done = bf16[3072,768]{1,0:T(8,128)(2,1)} async-done(((bf16[768,768]{1,0:T(8,128)(2,1)}), bf16[3072,768]{1,0:T(8,128)(2,1)}) %all-gather.15.cloned.1.call-update) | async-done | bytes 4718608 | tf_op jit(solution)/shard_map/all_gather | solution.py:256
  101.2 38.9 %all-gather.17.cloned.1.call-done = bf16[3072,768]{1,0:T(8,128)(2,1)} async-done(((bf16[768,768]{1,0:T(8,128)(2,1)}), bf16[3072,768]{1,0:T(8,128)(2,1)}) %all-gather.17.cloned.1.call-update) | async-done | bytes 4718608 | tf_op jit(solution)/shard_map/all_gather | solution.py:256
  140.1 55.0 %shard_map.255 = (bf16[1024,768]{1,0:T(8,128)(2,1)}, f32[1024,768]{1,0:T(8,128)}, bf16[1024,768]{1,0:T(8,128)(2,1)}, bf16[4,768,768]{2,1,0:T(8,128)(2,1)}, bf16[...) custom-call(bf16[1024,768]{1,0:T(8,128)(2,1)} %get-tuple-element.32.n2, ...), custom_call_target="tpu_custom_call" | custom-call | tf_op jit(solution)/shard_map/pallas_call | solution.py:245
  195.1 43.4 %shard_map.256 = (f32[1024,768]{1,0:T(8,128)}, bf16[3,768,768]{2,1,0:T(8,128)(2,1)}, f32[16,768]{1,0:T(8,128)}) custom-call(bf16[1024,768]{1,0:T(8,128)(2,1)} %constant_dynamic-slice_fusion.1.x, s32[1024,1]{1,0:T(8,128)} %copy.44.seg_col, s32[2,512]{1,0:T(2,128)} %reshape.71.seg_row, bf16[1024,768]{1,0:T(8,128)(2,1)} %get-tuple-element.36.normed, ...), custom_call_target="tpu_custom_call" | custom-call | tf_op jit(solution)/shard_map/pallas_call | solution.py:245
  238.5 2.4 copy.46
  240.9 1.0 copy-done.1
  242.2 8.9 %pad_maximum_fusion = bf16[4,2304,768]{2,1,0:T(8,128)(2,1)} fusion(bf16[4,576,768]{2,1,0:T(8,128)(2,1)S(1)} %bitcast.31, bf16[4,192,768]{2,1,0:T(8,128)(2,1)S(1)} %bitcast.38, bf16[4,768,768]{2,1,0:T(8,128)(2,1)} %get-tuple-element.47, bf16[4,768,768]{2,1,0:T(8,128)(2,1)S(1)} %copy-done.1), kind=kLoop, calls=%fused_computation | loop fusion | flops 56623104 | bytes 28311552 | tf_op jit(solution)/shard_map/concatenate | solution.py:307
  251.3 110.6 %reduce-scatter.2.cloned.1.call-done = bf16[1,2304,768]{2,1,0:T(8,128)(2,1)} async-done(((bf16[4,2304,768]{2,1,0:T(8,128)(2,1)}), bf16[1,2304,768]{2,1,0:T(8,128)(2,1)}) %reduce-scatter.2.cloned.1.call-update) | async-done | bytes 3538960 | tf_op jit(solution)/shard_map/reduce_scatter | solution.py:312
  361.9 43.2 %psum.14 = f32[16,768]{1,0:T(8,128)S(1)} all-reduce(f32[16,768]{1,0:T(8,128)S(1)} %add.20), channel_id=1, replica_groups=mesh['dp'=8,'mp'=4] {'dp','mp'}, use_global_device_ids=true, to_apply=%region_0.0 | all-reduce | flops 12288 | bytes 98304 | tf_op jit(solution)/shard_map/psum | solution.py:314
  405.2 0.7 dynamic-slice.2
  407.1 98.0 %all-reduce.2.cloned.1.call-done = bf16[2304,768]{1,0:T(8,128)(2,1)} async-done(((bf16[2304,768]{1,0:T(8,128)(2,1)}), bf16[2304,768]{1,0:T(8,128)(2,1)}) %all-reduce.2.cloned.1.call-update) | async-done | bytes 3538960 | tf_op jit(solution)/shard_map/psum | solution.py:313
  505.2 4.3 fusion
  509.5 1.3 slice.134
  510.8 0.9 slice.135
  (50 shorter events, 3.9 us)
Async XLA Ops:
  7.2 5.2 %copy-start.5 = (bf16[2,192]{1,0:T(2,128)(2,1)S(1)}, bf16[2,192]{1,0:T(2,128)(2,1)}, u32[]{:S(2)}) copy-start(bf16[2,192]{1,0:T(2,128)(2,1)} %param.20) | copy-start | bytes 2308
  7.2 5.3 %copy-start.7 = (bf16[192]{0:T(256)(128)(2,1)S(1)}, bf16[192]{0:T(256)(128)(2,1)}, u32[]{:S(2)}) copy-start(bf16[192]{0:T(256)(128)(2,1)} %param.17) | copy-start | bytes 1156
  7.2 5.3 %copy-start.8 = (bf16[192]{0:T(256)(128)(2,1)S(1)}, bf16[192]{0:T(256)(128)(2,1)}, u32[]{:S(2)}) copy-start(bf16[192]{0:T(256)(128)(2,1)} %param.18) | copy-start | bytes 1156
  7.2 5.3 %copy-start.9 = (bf16[192]{0:T(256)(128)(2,1)S(1)}, bf16[192]{0:T(256)(128)(2,1)}, u32[]{:S(2)}) copy-start(bf16[192]{0:T(256)(128)(2,1)} %param.22) | copy-start | bytes 1156
  7.2 5.3 %copy-start.10 = (bf16[192]{0:T(256)(128)(2,1)S(1)}, bf16[192]{0:T(256)(128)(2,1)}, u32[]{:S(2)}) copy-start(bf16[192]{0:T(256)(128)(2,1)} %param.23) | copy-start | bytes 1156
  7.2 5.3 %copy-start.11 = (bf16[192]{0:T(256)(128)(2,1)S(1)}, bf16[192]{0:T(256)(128)(2,1)}, u32[]{:S(2)}) copy-start(bf16[192]{0:T(256)(128)(2,1)} %param.24) | copy-start | bytes 1156
  7.2 5.3 %copy-start.6 = (bf16[768]{0:T(1024)(128)(2,1)S(1)}, bf16[768]{0:T(1024)(128)(2,1)}, u32[]{:S(2)}) copy-start(bf16[768]{0:T(1024)(128)(2,1)} %param.26) | copy-start | bytes 4612
  7.3 5.3 %copy-start.12 = (bf16[192]{0:T(256)(128)(2,1)S(1)}, bf16[192]{0:T(256)(128)(2,1)}, u32[]{:S(2)}) copy-start(bf16[192]{0:T(256)(128)(2,1)} %param.28) | copy-start | bytes 1156
  7.3 35.9 %all-gather.11.cloned.1.call-start = ((), (), s32[]{:S(2)}) async-start(), calls=%async_computation.3 | async-start | bytes 4423680 | tf_op jit(solution)/shard_map/all_gather | solution.py:256
  8.0 54.2 %all-gather.13.cloned.1.call-start = ((), (), s32[]{:S(2)}) async-start(), calls=%async_computation.4 | async-start | bytes 1474560 | tf_op jit(solution)/shard_map/all_gather | solution.py:256
  8.7 92.4 %all-gather.15.cloned.1.call-start = ((), (), s32[]{:S(2)}) async-start(), calls=%async_computation.5 | async-start | bytes 5898240 | tf_op jit(solution)/shard_map/all_gather | solution.py:256
  9.5 130.6 %all-gather.17.cloned.1.call-start = ((), (), s32[]{:S(2)}) async-start(), calls=%async_computation.6 | async-start | bytes 5898240 | tf_op jit(solution)/shard_map/all_gather | solution.py:256
  10.1 351.8 %reduce-scatter.2.cloned.1.call-start = ((), (), s32[]{:S(2)}) async-start(), calls=%async_computation.1 | async-start | bytes 17694720 | tf_op jit(solution)/shard_map/reduce_scatter | solution.py:312
  238.5 3.4 copy-start.1
  238.5 3.8 copy-start.2
  251.2 110.7 %copy-start.3 = (f32[16,768]{1,0:T(8,128)S(1)}, f32[16,768]{1,0:T(8,128)}, u32[]{:S(2)}) copy-start(f32[16,768]{1,0:T(8,128)} %get-tuple-element.44) | copy-start | bytes 147460
  251.2 110.7 %copy-start.4 = (f32[16,768]{1,0:T(8,128)S(1)}, f32[16,768]{1,0:T(8,128)}, u32[]{:S(2)}) copy-start(f32[16,768]{1,0:T(8,128)} %get-tuple-element.45) | copy-start | bytes 147460
  251.2 253.9 %all-reduce.2.cloned.1.call-start = ((), (), s32[]{:S(2)}) async-start(), calls=%async_computation.2 | async-start | bytes 7077888 | tf_op jit(solution)/shard_map/psum | solution.py:313
  505.2 4.3 copy-start
Sparse Core Ops, SparseCore 0:
  9.6 33.4 all-gather.10
  44.7 17.4 all-gather.12
  63.7 37.4 all-gather.14
  102.6 37.4 all-gather.16
  251.3 110.4 reduce-scatter.1
  365.3 139.7 all-reduce.1

commit v2 on v1

v2 whole, which is shorter than its diff:
```python
import functools

import jax
import jax.numpy as jnp
from jax import lax
from jax.experimental import pallas as pl
from jax.experimental.pallas import tpu as pltpu
from jax.sharding import PartitionSpec as P

HD = 64
LEN = 512
PIECE = 256
TILE = 256
F32 = jnp.float32
BF16 = jnp.bfloat16
MESH = pl.DeviceIdType.MESH
VMEM_LIMIT = 67043328
HBM = pl.BlockSpec(memory_space=pl.ANY)
VMEM = pl.BlockSpec(memory_space=pltpu.VMEM)


def nn(left, right):
    return jnp.dot(left, right, preferred_element_type=F32)


def nt(left, right):
    return lax.dot_general(left, right, (((1,), (1,)), ((), ())), preferred_element_type=F32)


def tn(left, right):
    return lax.dot_general(left, right, (((0,), (0,)), ((), ())), preferred_element_type=F32)


def ds(start, size, step=None):
    if isinstance(start, int):
        return pl.ds(start, size)
    return pl.ds(pl.multiple_of(start, step or size), size)


def rows_of(index, count):
    return ds(index * count, count)


def normal_of(values):
    centered = values - jnp.mean(values, axis=-1, keepdims=True)
    spread = jnp.mean(centered * centered, axis=-1, keepdims=True)
    inverse = lax.rsqrt(spread + 1e-06)
    return centered * inverse, inverse


def norm_input_back(normal, inverse, scaled):
    inner = jnp.mean(scaled * normal, axis=-1, keepdims=True)
    return inverse * (scaled - jnp.mean(scaled, axis=-1, keepdims=True) - normal * inner)


def column_sum(values):
    return jnp.sum(values, axis=0, keepdims=True)


def each(count, body):
    lax.fori_loop(0, count, lambda i, carry: (body(i), carry)[1], 0)


def at_steps(index, table):
    for step, actions in table.items():

        @pl.when(index == step)
        def _(actions=actions):
            for action in actions:
                action()


def add_into(target, *sources):
    rows = target.shape[0]
    tile = 64 if rows % 64 == 0 else 48

    def step(i):
        r = rows_of(i, tile)
        value = target[r, :].astype(F32)
        for source in sources:
            value += source[r, :].astype(F32)
        target[r, :] = value.astype(BF16)

    each(rows // tile, step)


def layer_kernel(
    dp, small_own, qkv_own, out_own, up_own, down_own, tokens, cot_hbm, segment,
    output, grad_x, feed_out, proj_out, qkv_out, vec_out, act_hbm, hidden_hbm,
    small, wqkv, w_out, w_up, w_down, x, cot, normed, qs, ks, vs, attended, n2, stats, hid, gup, act, bias,
    stat_rows, vec, vec_recv, fp, fcr, fyr, fxr, fzr, fer, op, ocr, oyr, oxr, ozr, oer, qp, qcr, qyr, qxr, qzr, qer,
    ag_local, ag_send, ag_recv, small_send, small_recv, local, act_sem, tile_a, tile_b, unit_send, unit_recv,
    vec_send, vec_got, credit, ready,
):
    me, d = lax.axis_index("mp"), lax.axis_index("dp")
    y, c = me // 2, me % 2
    count, width = x.shape
    part = width // 4
    half = width // 2
    sequences = count // LEN
    xb, zb = d % 2, (d // 2) % 2

    def across(bit):
        return d + bit - 2 * bit * ((d // bit) % 2)

    partner, above = (d, me + 1 - 2 * c), (d, me + 2 - 4 * y)
    diagonal = (d, 3 - me)
    side, level = (across(1), me), (across(2), me)
    far = [(across(bit), me) for bit in [1 << i for i in range(2, 12)] if bit < dp]
    peers = [partner, above, diagonal, side, level] + far
    barrier = pltpu.get_barrier_semaphore()
    for peer in peers:
        pl.semaphore_signal(barrier, inc=1, device_id=peer, device_id_type=MESH)
    pl.semaphore_wait(barrier, len(peers))

    def remote(source, target, send, recv, device):
        return pltpu.make_async_remote_copy(
            src_ref=source, dst_ref=target, send_sem=send, recv_sem=recv, device_id=device, device_id_type=MESH
        )

    def got(region, recv):
        remote(region, region, recv, recv, partner).wait_recv()

    def sent(region, send):
        remote(region, region, send, send, partner).wait_send()

    owns = (qkv_own, out_own, up_own, down_own)
    quarter = zb * 2 + xb
    q_side, q_level, q_diag = zb * 2 + 1 - xb, (1 - zb) * 2 + xb, 3 - quarter

    def own(t, q=None):
        if q is None:
            return owns[t]
        if t == 0:
            return qkv_own.at[:, rows_of(q, part // 4), :]
        rows = owns[t].shape[0] // 4
        return owns[t].at[rows_of(q, rows), :]

    def region(t, m, q=None):
        if t < 2:
            rows = part if q is None else part // 4
            start = m * part + (0 if q is None else q * rows)
            where = ds(start, rows, part // 4)
            return wqkv.at[:, where, :] if t == 0 else w_out.at[where, :]
        full = (w_up, w_down)[t - 2]
        if q is None:
            return full.at[m]
        rows = full.shape[1] // 4
        return full.at[m, rows_of(q, rows), :]

    m_core, m_y, m_diag = me + 1 - 2 * c, me + 2 - 4 * y, 3 - me
    through_side = (True, False, True, False)

    for i, peer in enumerate((diagonal, above, partner)):
        remote(small_own, small.at[me], small_send.at[i], small_recv.at[i], peer).start()
    pltpu.make_async_copy(small_own, small.at[me], local.at[0]).start()
    pltpu.make_async_copy(tokens.at[ds(me * count, count), :], x, local.at[1]).start()
    for t in range(4):
        remote(own(t, quarter), region(t, me, quarter), ag_send.at[t, 1], ag_recv.at[t, 1], above).start()
        pltpu.make_async_copy(own(t), region(t, me), ag_local.at[t]).start()
        remote(own(t), region(t, me), ag_send.at[t, 0], ag_recv.at[t, 0], partner).start()
    pltpu.make_async_copy(cot_hbm, cot, local.at[2]).start()

    def pass_on(t, q, k, device):
        where = region(t, m_y, q)
        remote(where, where, ag_send.at[t, k], ag_recv.at[t, k], device).start()

    def ag_y(t):
        got(region(t, m_y, quarter), ag_recv.at[t, 1])
        pass_on(t, quarter, 2, side)
        pass_on(t, quarter, 3, level)
        pass_on(t, quarter, 4, partner)

    def ag_side(t):
        got(region(t, m_y, q_side), ag_recv.at[t, 2])
        if not through_side[t]:
            pass_on(t, q_side, 7, level)
        pass_on(t, q_side, 5, partner)

    def ag_level(t):
        got(region(t, m_y, q_level), ag_recv.at[t, 3])
        if through_side[t]:
            pass_on(t, q_level, 7, side)
        pass_on(t, q_level, 6, partner)

    def ag_diag(t):
        got(region(t, m_y, q_diag), ag_recv.at[t, 7])
        pass_on(t, q_diag, 8, partner)

    def ag_near(t):
        pltpu.make_async_copy(own(t), region(t, me), ag_local.at[t]).wait()
        got(region(t, m_core), ag_recv.at[t, 0])

    def ag_rest(t):
        for k, q in ((4, quarter), (5, q_side), (6, q_level), (8, q_diag)):
            got(region(t, m_diag, q), ag_recv.at[t, k])

    def ag_sends(t):
        sent(own(t), ag_send.at[t, 0])
        sent(own(t, quarter), ag_send.at[t, 1])
        for k in range(2, 9):
            sent(own(t, quarter), ag_send.at[t, k])

    vec[...] = jnp.zeros_like(vec)
    for s in range(sequences):
        mine = segment[pl.ds(me * sequences + s, 1), :].astype(F32)
        column = jnp.broadcast_to(mine, (128, LEN)).T[:, :1]
        row_ids = lax.broadcasted_iota(jnp.int32, (LEN, LEN), 0)
        col_ids = lax.broadcasted_iota(jnp.int32, (LEN, LEN), 1)
        allowed = ((column == mine) & (mine != 0.0)) | (row_ids == col_ids)
        bias[s] = jnp.where(allowed, 0.0, -1e30)
        stats[rows_of(s, LEN), :] = jnp.zeros((LEN, 128), F32)
    pltpu.make_async_copy(small_own, small.at[me], local.at[0]).wait()
    for i, m in enumerate((m_diag, m_y, m_core)):
        got(small.at[m], small_recv.at[i])
    vectors = sum(small[m].astype(F32) for m in range(4))
    pltpu.make_async_copy(tokens.at[ds(0, count), :], x, local.at[1]).wait()
    g1, b1, b_query, b_value, b_out, g2, b2, b_down = (vectors[i : i + 1] for i in range(8))

    def ln_one(i):
        r = rows_of(i, TILE)
        normal, _ = normal_of(x[r, :].astype(F32))
        normed[r, :] = (normal * g1 + b1).astype(BF16)

    each(count // TILE, ln_one)
    lane = lax.broadcasted_iota(jnp.int32, (LEN, 128), 1)
    first = lane < HD
    pairs = half // 128
    small_sum = sum(small[m].astype(F32) for m in range(4))
    vec_recv[0] = small_sum

    def project(side_of):
        columns = ds(side_of * half, half, 128)

        def step(i):
            r = rows_of(i, LEN)
            value = normed[r, :]
            biases = vec_recv.at[0]
            query = nt(value, wqkv[0, columns, :]) + biases[2:3, columns]
            qs[r, columns] = (query.astype(BF16).astype(F32) * (HD**-0.5)).astype(BF16)
            ks[r, columns] = nt(value, wqkv[1, columns, :]).astype(BF16)
            vs[r, columns] = (nt(value, wqkv[2, columns, :]) + biases[3:4, columns]).astype(BF16)

        each(count // LEN, step)

    def attend(side_of, table):
        def step(i):
            s, p = i // pairs, side_of * pairs + i % pairs
            r, cols = rows_of(s, LEN), rows_of(p, 128)
            q2, k2, v2 = qs[r, cols], ks[r, cols], vs[r, cols]
            results = []
            kept = stats[r, :]
            for part_of in range(2):
                mine = first if part_of == 0 else ~first
                scores = nt(jnp.where(mine, q2, jnp.zeros_like(q2)), k2) + bias[s]
                top = jnp.max(scores, axis=-1, keepdims=True)
                expo = jnp.exp(scores - top)
                total = jnp.sum(expo, axis=-1, keepdims=True)
                results.append(nn(expo.astype(BF16), v2) * (1.0 / total))
                kept = jnp.where(lane == 2 * p + part_of, top + jnp.log(total), kept)
            stats[r, :] = kept
            attended[r, cols] = jnp.where(first, results[0], results[1]).astype(BF16)
            at_steps(i, table)

        each(sequences * pairs, step)

    def run(function, *args):
        return functools.partial(function, *args)

    ag_near(0)
    project(y)
    attend(
        y,
        {
            0: [run(ag_y, 0), run(ag_y, 1)],
            3: [run(ag_level, 0), run(ag_side, 0)],
            4: [run(ag_side, 1), run(ag_level, 1)],
            5: [run(ag_y, 2)],
        },
    )
    ag_diag(0)
    ag_rest(0)
    project(1 - y)
    attend(
        1 - y,
        {
            0: [run(ag_diag, 1), run(ag_y, 3)],
            2: [run(ag_side, 2), run(ag_level, 2)],
            5: [run(ag_side, 3), run(ag_level, 3), run(ag_diag, 2)],
        },
    )
    ag_near(1)
    ag_rest(1)

    def out_step(i):
        r = rows_of(i, TILE)
        value = x[r, :].astype(F32) + nn(attended[r, :], w_out[...]) + vec_recv[0, 4:5, :]
        hid[r, :] = value
        pltpu.make_async_copy(hid.at[r, :], hidden_hbm.at[r, :], tile_a.at[i]).start()
        normal, _ = normal_of(value)
        n2[r, :] = (normal * vec_recv[0, 5:6, :] + vec_recv[0, 6:7, :]).astype(BF16)

    each(count // TILE, out_step)
    ag_near(2)
    ag_rest(2)
    ag_diag(3)
    ag_near(3)
    ag_rest(3)
    pltpu.make_async_copy(cot_hbm, cot, local.at[2]).wait()

    up_bias = vec_recv.at[0]
    feed_slots = 2

    def unit(u, kept, cr, yr, xr, zr, er):
        rows = kept.shape[0]
        return (u, rows, kept, cr, yr, xr, zr, er)

    def own_half(rows):
        return ds(xb * (rows // 2), rows // 2, rows // 4)

    def other_half(rows):
        return ds((1 - xb) * (rows // 2), rows // 2, rows // 4)

    def own_quarter(rows):
        return ds(xb * (rows // 2) + zb * (rows // 4), rows // 4)

    def other_quarter(rows):
        return ds(xb * (rows // 2) + (1 - zb) * (rows // 4), rows // 4)

    def send_unit(u, k, source, target, device):
        remote(source, target, unit_send.at[u, k], unit_recv.at[u, k], device).start()

    def take_sum(unit_of):
        u, rows, kept, cr, yr, xr, zr, er = unit_of
        got(cr, unit_recv.at[u, 2])
        got(yr, unit_recv.at[u, 1])
        add_into(kept, cr, yr)
        send_unit(u, 3, kept.at[other_half(rows), :], xr, side)

    def far_room(unit_of, i):
        u, rows, kept, cr, yr, xr, zr, er = unit_of
        return er if i == 0 else cr.at[(i - 1) * (rows // 4) : i * (rows // 4), :]

    def send_far(unit_of, i):
        u, rows, kept, cr, yr, xr, zr, er = unit_of
        if i > 0:
            pl.semaphore_wait(ready.at[u, 2 + i], 1)
        send_unit(u, 7 + i, kept.at[own_quarter(rows), :], far_room(unit_of, i), far[i])

    def take_side(unit_of):
        u, rows, kept, cr, yr, xr, zr, er = unit_of
        for i in range(1, len(far)):
            pl.semaphore_signal(ready.at[u, 2 + i], inc=1, device_id=far[i], device_id_type=MESH)
        got(xr, unit_recv.at[u, 3])
        sent(xr, unit_send.at[u, 3])
        pl.semaphore_signal(ready.at[u, 0], inc=1, device_id=side, device_id_type=MESH)
        add_into(kept.at[own_half(rows), :], xr)
        send_unit(u, 4, kept.at[other_quarter(rows), :], zr, level)

    def give_level(unit_of):
        u, rows, kept, cr, yr, xr, zr, er = unit_of
        mine = kept.at[own_quarter(rows), :]
        pl.semaphore_wait(ready.at[u, 1], 1)
        send_unit(u, 5, mine, mine, level)

    def take_level(unit_of):
        u, rows, kept, cr, yr, xr, zr, er = unit_of
        got(zr, unit_recv.at[u, 4])
        sent(zr, unit_send.at[u, 4])
        pl.semaphore_signal(ready.at[u, 1], inc=1, device_id=level, device_id_type=MESH)
        mine = kept.at[own_quarter(rows), :]
        add_into(mine, zr)
        if far:
            send_far(unit_of, 0)
        else:
            give_level(unit_of)

    def take_far(unit_of):
        u, rows, kept, cr, yr, xr, zr, er = unit_of
        mine = kept.at[own_quarter(rows), :]
        for i, _ in enumerate(far):
            landed = far_room(unit_of, i)
            got(landed, unit_recv.at[u, 7 + i])
            sent(mine, unit_send.at[u, 7 + i])
            add_into(mine, landed)
            if i + 1 < len(far):
                send_far(unit_of, i + 1)
        if far:
            give_level(unit_of)

    def give_side(unit_of):
        u, rows, kept, cr, yr, xr, zr, er = unit_of
        got(kept.at[other_quarter(rows), :], unit_recv.at[u, 5])
        mine = kept.at[own_half(rows), :]
        pl.semaphore_wait(ready.at[u, 0], 1)
        send_unit(u, 6, mine, mine, side)

    def finish(unit_of, target, sem):
        u, rows, kept, cr, yr, xr, zr, er = unit_of
        got(kept.at[other_half(rows), :], unit_recv.at[u, 6])
        pltpu.make_async_copy(kept, target, sem).start()

    def unit_sends(unit_of):
        u, rows, kept, cr, yr, xr, zr, er = unit_of
        sent(kept, unit_send.at[u, 1])
        sent(kept.at[own_half(rows), :], unit_send.at[u, 6])
        sent(kept.at[own_quarter(rows), :], unit_send.at[u, 5])

    feeds = [
        unit(s, fp.at[feed_slots + 3 + s], fcr.at[s], fyr.at[s], fxr.at[s], fzr.at[s], fer.at[s]) for s in range(3)
    ]
    proj = unit(3, op.at[3], ocr, oyr, oxr, ozr, oer)
    attn = unit(4, qp.at[2], qcr, qyr, qxr, qzr, qer)

    def feed_first(sub, slot):
        send_unit(sub, 0, fp.at[slot], fcr.at[sub], partner)

    def feed_second(sub, slot):
        got(fcr.at[sub], unit_recv.at[sub, 0])
        add_into(fp.at[slot], fcr.at[sub])
        pl.semaphore_signal(credit, inc=1, device_id=partner, device_id_type=MESH)
        send_unit(sub, 1, fp.at[slot], fyr.at[sub], above)

    def feed_third(sub, slot):
        pl.semaphore_wait(credit, 1)
        send_unit(sub, 2, fp.at[slot], fcr.at[sub], partner)

    steps = 12

    def feed_step(i):
        late, odd, sub = i // 6, i % 2, (i % 6) // 2
        m = 2 * jnp.where(late == 0, 1 - y, y) + jnp.where(odd == 0, 1 - c, c)
        slot = jnp.where(odd == 0, (i // 2) % feed_slots, feed_slots + 3 * late + sub)
        cols = rows_of(sub, PIECE)
        whole = rows_of(m * 3 + sub, PIECE)
        wu, wd = w_up[m, :, cols], w_down[m, cols, :]
        piece_bias = up_bias[pl.ds(8 + m, 1), cols]
        buffer = i % 2

        @pl.when(i >= 2)
        def _():
            pltpu.make_async_copy(act.at[buffer], act_hbm.at[:, whole], act_sem.at[buffer]).wait()

        @pl.when((i >= 4) & (odd == 0))
        def _():
            before = i - 4
            sent(fp.at[slot], unit_send.at[(before % 6) // 2, 2 * (before // 6)])

        def rows_step(j):
            r = rows_of(j, LEN)
            up = nn(n2[r, :], wu) + piece_bias
            half_cdf = 0.5 * (1.0 + lax.erf(up * (0.5**0.5)))
            slope = half_cdf + up * (jnp.exp(-0.5 * up * up) * 0.3989422804014327)
            act[buffer, r, :] = (up * half_cdf).astype(BF16)
            grad = (nt(cot[r, :], wd) * slope).astype(BF16)
            gup[r, whole] = grad
            vec[pl.ds(8 + m, 1), cols] += column_sum(grad.astype(F32))

        each(count // LEN, rows_step)
        pltpu.make_async_copy(act.at[buffer], act_hbm.at[:, whole], act_sem.at[buffer]).start()
        fp[slot, :PIECE, :] = tn(act[buffer], cot[...]).astype(BF16)
        fp[slot, PIECE:, :] = tn(gup[:, whole], n2[...]).astype(BF16)

        @pl.when((late == 0) & (odd == 0))
        def _():
            feed_first(sub, slot)

        @pl.when((late == 0) & (odd == 1))
        def _():
            feed_second(sub, slot)

        @pl.when((late == 1) & (odd == 0))
        def _():
            feed_third(sub, slot)

        at_steps(i, {7: [run(take_sum, feeds[0])], 10: [run(take_side, feeds[0])], 11: [run(take_sum, feeds[1])]})

    vec[8:16, :] = jnp.zeros_like(vec[8:16, :])
    each(steps, feed_step)
    for buffer in range(2):
        pltpu.make_async_copy(act.at[buffer], act_hbm.at[:, ds(0, PIECE)], act_sem.at[buffer]).wait()
    for i in range(count // TILE):
        r = rows_of(i, TILE)
        pltpu.make_async_copy(hid.at[r, :], hidden_hbm.at[r, :], tile_a.at[i]).wait()

    def hidden_step(i):
        r = rows_of(i, TILE)
        incoming = nt(gup[r, :width], w_up[0])
        for m in range(1, 4):
            incoming += nt(gup[r, m * width : (m + 1) * width], w_up[m])
        normal, inverse = normal_of(hid[r, :])
        wide = cot[r, :].astype(F32)
        grad = wide + norm_input_back(normal, inverse, incoming * vec_recv[0, 5:6, :])
        hid[r, :] = grad
        vec[4:5, :] += column_sum(grad)
        vec[5:6, :] += column_sum(incoming * normal)
        vec[6:7, :] += column_sum(incoming)
        vec[7:8, :] += column_sum(wide)
        narrow = grad.astype(BF16)
        gup[r, 3 * width :] = narrow
        n2[r, :] = nt(narrow, w_out[...]).astype(BF16)
        at_steps(i, {0: [run(take_level, feeds[0])], 3: [run(take_far, feeds[0]), run(take_side, feeds[1])]})

    each(count // TILE, hidden_step)
    product = tn(attended[...], gup[:, 3 * width :])
    for m in range(4):
        slot = 2 * jnp.where(y == m // 2, 1, 0) + jnp.where(c == m % 2, 1, 0)
        op[slot] = product[m * part : (m + 1) * part, :].astype(BF16)
    send_unit(3, 0, op.at[0], ocr, partner)

    def proj_second():
        got(ocr, unit_recv.at[3, 0])
        add_into(op.at[1], ocr)
        pl.semaphore_signal(credit, inc=1, device_id=partner, device_id_type=MESH)
        send_unit(3, 1, op.at[1], oyr, above)

    def proj_third():
        pl.semaphore_wait(credit, 1)
        send_unit(3, 2, op.at[2], ocr, partner)

    def attend_back(side_of, table):
        def step(i):
            s, p = i // pairs, side_of * pairs + i % pairs
            r, cols = rows_of(s, LEN), rows_of(p, 128)

            @pl.when(i % pairs == 0)
            def _():
                stat_rows[...] = stats[r, :].T

            q2, k2, v2, d2 = qs[r, cols], ks[r, cols], vs[r, cols], n2[r, cols]
            rq, rk, rv = 0.0, 0.0, 0.0
            for part_of in range(2):
                mine = first if part_of == 0 else ~first
                qm = jnp.where(mine, q2, jnp.zeros_like(q2))
                km = jnp.where(mine, k2, jnp.zeros_like(k2))
                dm = jnp.where(mine, d2, jnp.zeros_like(d2))
                probs = jnp.exp(nt(k2, qm) + bias[s] - stat_rows[pl.ds(2 * p + part_of, 1), :])
                grad_probs = nt(v2, dm)
                inner = jnp.sum(probs * grad_probs, axis=0, keepdims=True)
                grad_scores = (probs * (grad_probs - inner)).astype(BF16)
                rv += nn(probs.astype(BF16), dm)
                rk += nn(grad_scores, qm)
                rq += tn(grad_scores, km)
            gup[r, cols] = (rq * (HD**-0.5)).astype(BF16)
            gup[r, ds(width + p * 128, 128)] = rk.astype(BF16)
            gup[r, ds(2 * width + p * 128, 128)] = rv.astype(BF16)
            at_steps(i, table)

        each(sequences * pairs, step)

    def weight_of_half(side_of, kept_slot):
        for k in range(3):
            grads = gup[:, ds(k * width + side_of * half, half, 128)]
            product = tn(grads, normed[...]).astype(BF16)
            for core in range(2):
                slot = jnp.where(c == core, kept_slot, 0)
                qp[slot, k * part : (k + 1) * part, :] = product[core * part : (core + 1) * part, :]

    attend_back(
        1 - y,
        {
            0: [proj_second, run(give_side, feeds[0]), run(take_level, feeds[1])],
            1: [proj_third, run(take_sum, feeds[2])],
            3: [run(finish, feeds[0], feed_out.at[0], local.at[3]), run(take_far, feeds[1]), run(take_sum, proj)],
            4: [run(take_side, feeds[2])],
            5: [run(give_side, feeds[1]), run(take_side, proj)],
        },
    )
    weight_of_half(1 - y, 1)
    send_unit(4, 0, qp.at[0], qcr, partner)

    def attn_second():
        got(qcr, unit_recv.at[4, 0])
        add_into(qp.at[1], qcr)
        pl.semaphore_signal(credit, inc=1, device_id=partner, device_id_type=MESH)
        send_unit(4, 1, qp.at[1], qyr, above)

    attend_back(
        y,
        {
            0: [attn_second, run(take_level, feeds[2])],
            1: [run(take_level, proj)],
            2: [run(take_far, feeds[2])],
            3: [run(finish, feeds[1], feed_out.at[1], local.at[4]), run(take_far, proj), run(give_side, feeds[2])],
            5: [run(give_side, proj), run(finish, feeds[2], feed_out.at[2], local.at[5])],
        },
    )
    sent(qp.at[0], unit_send.at[4, 0])
    weight_of_half(y, 2)
    pl.semaphore_wait(credit, 1)
    send_unit(4, 2, qp.at[0], qcr, partner)

    def input_step(i):
        r = rows_of(i, TILE)
        q, k, v = gup[r, :width], gup[r, width : 2 * width], gup[r, 2 * width : 3 * width]
        incoming = nn(q, wqkv[0]) + nn(k, wqkv[1]) + nn(v, wqkv[2])
        normal, inverse = normal_of(x[r, :].astype(F32))
        hid[r, :] += norm_input_back(normal, inverse, incoming * vec_recv[0, 0:1, :])
        vec[0:1, :] += column_sum(incoming * normal)
        vec[1:2, :] += column_sum(incoming)
        vec[2:3, :] += column_sum(q.astype(F32))
        vec[3:4, :] += column_sum(v.astype(F32))
        pltpu.make_async_copy(hid.at[r, :], grad_x.at[r, :], tile_a.at[i]).start()
        pltpu.make_async_copy(act_hbm.at[r, :], gup.at[r, :], tile_b.at[i]).start()
        at_steps(i, {0: [run(take_sum, attn)], 3: [run(finish, proj, proj_out, local.at[6])]})

    each(count // TILE, input_step)

    def reload(i):
        r = rows_of(i, TILE)
        pltpu.make_async_copy(hid.at[r, :], grad_x.at[r, :], tile_a.at[i]).wait()
        pltpu.make_async_copy(hidden_hbm.at[r, :], hid.at[r, :], tile_a.at[i]).start()

    each(count // TILE, reload)
    b_down = vec_recv[0, 7:8, :]

    rounds = [partner, above, side, level] + far

    def vec_start(i):
        remote(vec, vec_recv.at[1 + i], vec_send.at[i], vec_got.at[i], rounds[i]).start()

    def vec_step(i):
        got(vec_recv.at[1 + i], vec_got.at[i])
        sent(vec, vec_send.at[i])
        vec[...] += vec_recv[1 + i]
        if i + 1 < len(rounds):
            vec_start(i + 1)

    vec_start(0)

    def output_step(i):
        r = rows_of(i, TILE)
        pltpu.make_async_copy(hidden_hbm.at[r, :], hid.at[r, :], tile_a.at[i]).wait()
        pltpu.make_async_copy(act_hbm.at[r, :], gup.at[r, :], tile_b.at[i]).wait()
        result = hid[r, :] + b_down
        for m in range(4):
            result += nn(gup[r, m * width : (m + 1) * width], w_down[m])
        x[r, :] = result.astype(BF16)
        pltpu.make_async_copy(x.at[r, :], output.at[r, :], tile_a.at[i]).start()
        at_steps(
            i,
            {
                0: [run(vec_step, 0)],
                1: [run(vec_step, 1)],
                2: [run(take_side, attn), run(vec_step, 2)],
                3: [run(vec_step, 3)],
            },
        )

    each(count // TILE, output_step)
    take_level(attn)
    for i in range(4, len(rounds)):
        vec_step(i)
    pltpu.make_async_copy(vec, vec_out, local.at[7]).start()
    take_far(attn)
    give_side(attn)
    finish(attn, qkv_out, local.at[8])

    for i in range(3):
        sent(small_own, small_send.at[i])
    for t in range(4):
        ag_sends(t)
    for k, slot in ((1, 0), (2, 1)):
        sent(fp.at[slot], unit_send.at[k, 2])
    for k in (0, 2):
        sent(op.at[0], unit_send.at[3, k])
    sent(qp.at[0], unit_send.at[4, 2])
    for unit_of in feeds + [proj, attn]:
        unit_sends(unit_of)
    for i in range(count // TILE):
        r = rows_of(i, TILE)
        pltpu.make_async_copy(x.at[r, :], output.at[r, :], tile_a.at[i]).wait()
    for s in range(3):
        pltpu.make_async_copy(feeds[s][2], feed_out.at[s], local.at[3 + s]).wait()
    pltpu.make_async_copy(op.at[3], proj_out, local.at[6]).wait()
    pltpu.make_async_copy(vec, vec_out, local.at[7]).wait()
    pltpu.make_async_copy(qp.at[2], qkv_out, local.at[8]).wait()


def per_device(
    dp, tokens, segment, ln1_gain, ln1_bias, w_qkv, b_qv, w_out, b_out, ln2_gain, ln2_bias, w_up, b_up, w_down, b_down,
    cotangent,
):
    mp = 4
    me = lax.axis_index("mp")
    count, width = cotangent.shape
    part = width // mp
    feed = w_up.shape[1]
    bits = dp.bit_length() - 1
    far = bits - 2
    pieces = jnp.stack([ln1_gain, ln1_bias, b_qv[0], b_qv[1], b_out, ln2_gain, ln2_bias, b_down])
    small_own = lax.dynamic_update_slice(jnp.zeros((16, width), BF16), pieces, (0, me * part))
    small_own = lax.dynamic_update_slice(small_own, b_up.reshape(1, feed), (8 + me, 0))
    qkv_own = w_qkv.swapaxes(1, 2)

    def shape(*dims, kind=BF16):
        return jax.ShapeDtypeStruct(dims, kind)

    def room(*dims, kind=BF16):
        return pltpu.VMEM(dims, kind)

    unit_rows = 2 * PIECE
    dma = pltpu.SemaphoreType.DMA
    outs = [
        shape(count, width), shape(count, width, kind=F32), shape(3, unit_rows, width), shape(part, width),
        shape(3 * part, width), shape(16, width, kind=F32), shape(count, mp * feed), shape(count, width, kind=F32),
    ]

    def unit_rooms(rows, slots, lead):
        return [
            room(slots, rows, width), room(*lead, rows, width), room(*lead, rows, width),
            room(*lead, rows // 2, width), room(*lead, rows // 4, width), room(*lead, rows // 4, width),
        ]

    scratch = [
        room(mp, 16, width), room(3, width, width), room(width, width), room(mp, width, feed), room(mp, feed, width),
        *[room(count, width) for _ in range(8)],
        room(count, 128, kind=F32), room(count, width, kind=F32), room(count, mp * feed), room(2, count, PIECE),
        room(count // LEN, LEN, LEN, kind=F32), room(128, LEN, kind=F32), room(16, width, kind=F32),
        room(1 + 2 + bits, 16, width, kind=F32),
        *unit_rooms(unit_rows, 8, (3,)), *unit_rooms(part, 4, ()), *unit_rooms(3 * part, 3, ()),
        dma((4,)), dma((4, 9)), dma((4, 9)), dma((3,)), dma((3,)), dma((9,)), dma((2,)), dma((4,)), dma((4,)),
        dma((5, 7 + max(far, 1))), dma((5, 7 + max(far, 1))), dma((2 + bits,)), dma((2 + bits,)),
        pltpu.SemaphoreType.REGULAR, pltpu.SemaphoreType.REGULAR((5, 2 + max(far, 1))),
    ]
    args = (
        small_own, qkv_own, w_out, w_up, w_down, tokens, cotangent, segment.reshape(-1, LEN),
    )
    results = pl.pallas_call(
        functools.partial(layer_kernel, dp),
        out_shape=outs,
        in_specs=[HBM] * 7 + [VMEM],
        out_specs=[HBM] * len(outs),
        scratch_shapes=scratch,
        compiler_params=pltpu.CompilerParams(
            vmem_limit_bytes=VMEM_LIMIT, collective_id=0, has_side_effects=True
        ),
    )(*args)
    output, grad_x, feeds, proj, attn, vec = results[:6]
    eight = lax.dynamic_slice_in_dim(vec[:8], me * part, part, 1)
    grad_b_up = lax.dynamic_slice_in_dim(vec, 8 + me, 1, 0).reshape(-1)
    g_down = feeds[:, :PIECE].reshape(feed, width).astype(F32)
    g_up = feeds[:, PIECE:].reshape(feed, width).T.astype(F32)
    g_qkv = attn.reshape(3, part, width).swapaxes(1, 2).astype(F32)
    return (
        output, grad_x, eight[0], eight[1], g_qkv, eight[2:4], proj.astype(F32), eight[4], eight[5], eight[6],
        g_up, grad_b_up, g_down, eight[7],
    )


def solution(mesh):
    rows = P(("dp", "mp"), None)
    return jax.shard_map(
        functools.partial(per_device, mesh.shape["dp"]),
        mesh=mesh,
        in_specs=(
            P("dp", None), P("dp"), P("mp"), P("mp"), P(None, None, "mp"), P(None, "mp"), P("mp", None), P("mp"),
            P("mp"), P("mp"), P(None, "mp"), P("mp"), P("mp", None), P("mp"), rows,
        ),
        out_specs=(
            rows, rows, P("mp"), P("mp"), P(None, None, "mp"), P(None, "mp"), P("mp", None), P("mp"), P("mp"), P("mp"),
            P(None, "mp"), P("mp"), P("mp", None), P("mp"),
        ),
        check_vma=False,
    )
```

time: 519 us -> 248 us (0.48)
  waiting for transfers between devices: 291 us -> 0 us
  Pallas kernels: 128 us -> 222 us
  blocking collectives: 49.5 us -> 0 us
  between operations: 14.4 us -> 0.68 us
  other arithmetic: 9.56 us -> 4.12 us
  local copies, waits for them, and re-layouts: 26.2 us -> 21 us
    reduce_scatter x1 -> x0, waiting for transfers between devices: 111 us -> none  [per_device(): share = lax.psum_scatter(packed, 'mp', scatter_dimension=0, tiled=False)]
    psum x1 -> x0, waiting for transfers between devices: 98 us -> none  [per_device(): share = lax.psum(share, 'dp').astype(F32)]
    pallas_call x3 -> x1, Pallas kernels: 128 us -> 222 us  [per_device(): pl.pallas_call(functools.partial(layer_kernel, dp), out_shape=outs, in_sp...]
    all_gather x4 -> x0, waiting for transfers between devices: 79.8 us -> none  [gathered(): return lax.all_gather(value, 'mp', axis=0)]
    psum x1 -> x0, blocking collectives: 43.2 us -> none  [per_device(): vec = lax.psum(vec_a + vec_b, ('dp', 'mp'))]
    slice x14 -> x1, local copies, waits for them, and re-layouts: 11.2 us -> 1.79 us  [per_device(): g_down = feeds[:, :PIECE].reshape(feed, width).astype(F32)]
    concatenate x1 -> x0, other arithmetic: 8.94 us -> none  [per_device(): jnp.concatenate([gw_down, gw_up, gw_out.reshape(mp, part, width), gw_qkv....]
    all_gather x1 -> x0, blocking collectives: 6.23 us -> none  [gathered(): return lax.all_gather(value, 'mp', axis=0)]
  transfers between devices with their start and end apart: 6 -> 0, of which waited for: 6 -> 0; matrix products, arithmetic and copies ran while one was open for 3% -> 0% of each run, Pallas kernels for 6% -> 0%
where the time goes in v2:
time: 248 us
  Pallas kernels  222 us (90%)
  local copies, waits for them, and re-layouts  21 us (8%)
  other arithmetic  4.12 us (2%)
    pallas_call x1, Pallas kernels, per_device(): pl.pallas_call(functools.partial(layer_kernel, dp), out_shape=outs, in_sp...  222 us

profile of v2, /device:TPU:0, one launch (start us, length us, event | category | flops | bytes accessed | tf_op | source)
XLA Modules:
  0.0 247.7 jit_solution(8722682490814187270)
XLA Ops:
  0.7 0.7 stack.22
  1.3 0.7 stack.23
  2.0 0.7 stack.24
  2.6 0.7 stack.25
  3.3 0.7 stack.26
  3.9 0.7 stack.27
  4.6 0.7 stack.28
  5.3 0.6 broadcast_in_dim.3
  5.9 2.6 %dynamic_update_slice.6 = bf16[16,768]{1,0:T(8,128)(2,1)} dynamic-update-slice(bf16[16,768]{1,0:T(8,128)(2,1)} %broadcast_in_dim.3, bf16[8,192]{1,0:T(8,128)(2,1)S(1)} %stack.28, s32[]{:T(128)} %constant.2.clone.1, s32[]{:T(128)S(6)} %select_n.8) | dynamic-update-slice | bytes 6148 | tf_op jit(solution)/shard_map/dynamic_update_slice | solution.py:692
  8.5 0.7 reshape.46
  9.2 1.3 dynamic_update_slice.7.small_own
  10.5 1.3 reshape.47.segment
  11.8 221.9 %shard_map.254 = (bf16[1024,768]{1,0:T(8,128)(2,1)}, f32[1024,768]{1,0:T(8,128)}, bf16[3,512,768]{2,1,0:T(8,128)(2,1)}, bf16[192,768]{1,0:T(8,128)(2,1)}, bf16[5...) custom-call(bf16[16,768]{1,0:T(8,128)(2,1)} %dynamic_update_slice.7.small_own, ...), custom_call_target="tpu_custom_call" | custom-call | tf_op jit(solution)/shard_map/pallas_call | solution.py:729
  233.8 1.8 fusion
  235.6 1.9 bitcast_convert_fusion
  237.5 0.0 copy-start.4
  237.5 0.0 copy-start.2
  237.5 1.9 copy.29
  239.4 0.0 copy-start.3
  239.4 0.0 copy-done.4
  239.4 0.7 fusion.1
  240.1 0.7 dynamic-slice.2
  240.8 0.6 dynamic-slice_reduce_fusion
  241.4 0.0 copy-done.2
  241.4 0.0 copy-start.1
  241.4 1.4 convert_bitcast_fusion
  242.7 0.0 copy-done.3
  242.7 0.9 convert_element_type.30
  243.6 0.0 copy-done.1
  243.6 1.1 copy.34
  244.7 1.3 copy-done
  246.0 1.7 copy.35
  (2 shorter events, 0.0 us)
Async XLA Ops:
  237.5 2.0 copy-start.4
  237.5 3.9 %copy-start.2 = (bf16[576,768]{1,0:T(8,128)(2,1)S(1)}, bf16[576,768]{1,0:T(8,128)(2,1)}, u32[]{:S(2)}) copy-start(bf16[576,768]{1,0:T(8,128)(2,1)} %get-tuple-element.23) | copy-start | bytes 2654212
  239.4 3.3 %copy-start.3 = (bf16[192,768]{1,0:T(8,128)(2,1)S(1)}, bf16[192,768]{1,0:T(8,128)(2,1)}, u32[]{:S(2)}) copy-start(bf16[192,768]{1,0:T(8,128)(2,1)} %get-tuple-element.24) | copy-start | bytes 884740
  241.4 2.2 copy-start.1
  243.6 2.5 copy-start

commit v3 on v2

--- a/solution.py
+++ b/solution.py
@@ -87,8 +87,8 @@
 def layer_kernel(
     dp, small_own, qkv_own, out_own, up_own, down_own, tokens, cot_hbm, segment,
     output, grad_x, feed_out, proj_out, qkv_out, vec_out, act_hbm, hidden_hbm,
-    small, wqkv, w_out, w_up, w_down, x, cot, normed, qs, ks, vs, attended, n2, stats, hid, gup, act, bias,
-    stat_rows, vec, vec_recv, fp, fcr, fyr, fxr, fzr, fer, op, ocr, oyr, oxr, ozr, oer, qp, qcr, qyr, qxr, qzr, qer,
+    small, wqkv, w_out, w_up, w_down, x, cot, normed, qs, ks, vs, attended, n2, hid, gup, act, bias,
+    stat_rows, vec, vec_recv, fp, fcr, fyr, fxr, op, ocr, oyr, oxr,
     ag_local, ag_send, ag_recv, small_send, small_recv, local, act_sem, tile_a, tile_b, unit_send, unit_recv,
     vec_send, vec_got, credit, ready,
 ):
@@ -124,38 +124,41 @@
     def sent(region, send):
         remote(region, region, send, send, partner).wait_send()
 
-    owns = (qkv_own, out_own, up_own, down_own)
     quarter = zb * 2 + xb
     q_side, q_level, q_diag = zb * 2 + 1 - xb, (1 - zb) * 2 + xb, 3 - quarter
+    tensors = 4 + 2 * (w_up.shape[2] // PIECE)
+    q_in, k_in, v_in, o_in = range(4)
+    ups, downs = range(4, tensors, 2), range(5, tensors, 2)
+
+    def window(ref, t, q, start):
+        piece = (t - 4) // 2 * PIECE
+        if t in ups:
+            rows = width if q is None else width // 4
+            return ref.at[*start, ds(0 if q is None else q * rows, rows), ds(piece, PIECE)]
+        rows = PIECE if q is None else PIECE // 4
+        return ref.at[*start, ds(piece + (0 if q is None else q * rows), rows, PIECE // 4), :]
 
     def own(t, q=None):
-        if q is None:
-            return owns[t]
-        if t == 0:
-            return qkv_own.at[:, rows_of(q, part // 4), :]
-        rows = owns[t].shape[0] // 4
-        return owns[t].at[rows_of(q, rows), :]
+        if t > o_in:
+            return window(up_own if t in ups else down_own, t, q, ())
+        rows = ds(0, part) if q is None else rows_of(q, part // 4)
+        return out_own.at[rows, :] if t == o_in else qkv_own.at[t, rows, :]
 
     def region(t, m, q=None):
-        if t < 2:
-            rows = part if q is None else part // 4
-            start = m * part + (0 if q is None else q * rows)
-            where = ds(start, rows, part // 4)
-            return wqkv.at[:, where, :] if t == 0 else w_out.at[where, :]
-        full = (w_up, w_down)[t - 2]
-        if q is None:
-            return full.at[m]
-        rows = full.shape[1] // 4
-        return full.at[m, rows_of(q, rows), :]
+        if t > o_in:
+            return window(w_up if t in ups else w_down, t, q, (m,))
+        rows = part if q is None else part // 4
+        where = ds(m * part + (0 if q is None else q * rows), rows, part // 4)
+        return w_out.at[where, :] if t == o_in else wqkv.at[t, where, :]
 
     m_core, m_y, m_diag = me + 1 - 2 * c, me + 2 - 4 * y, 3 - me
-    through_side = (True, False, True, False)
+    through_side = [t in (q_in, v_in) or t in ups for t in range(tensors)]
 
     for i, peer in enumerate((diagonal, above, partner)):
         remote(small_own, small.at[me], small_send.at[i], small_recv.at[i], peer).start()
     pltpu.make_async_copy(small_own, small.at[me], local.at[0]).start()
     pltpu.make_async_copy(tokens.at[ds(me * count, count), :], x, local.at[1]).start()
-    for t in range(4):
+    for t in range(tensors):
         remote(own(t, quarter), region(t, me, quarter), ag_send.at[t, 1], ag_recv.at[t, 1], above).start()
         pltpu.make_async_copy(own(t), region(t, me), ag_local.at[t]).start()
         remote(own(t), region(t, me), ag_send.at[t, 0], ag_recv.at[t, 0], partner).start()
@@ -209,7 +212,7 @@
         col_ids = lax.broadcasted_iota(jnp.int32, (LEN, LEN), 1)
         allowed = ((column == mine) & (mine != 0.0)) | (row_ids == col_ids)
         bias[s] = jnp.where(allowed, 0.0, -1e30)
-        stats[rows_of(s, LEN), :] = jnp.zeros((LEN, 128), F32)
+        hid[rows_of(s, LEN), :128] = jnp.zeros((LEN, 128), F32)
     pltpu.make_async_copy(small_own, small.at[me], local.at[0]).wait()
     for i, m in enumerate((m_diag, m_y, m_core)):
         got(small.at[m], small_recv.at[i])
@@ -229,7 +232,7 @@
     small_sum = sum(small[m].astype(F32) for m in range(4))
     vec_recv[0] = small_sum
 
-    def project(side_of):
+    def project(side_of, table):
         columns = ds(side_of * half, half, 128)
 
         def step(i):
@@ -240,6 +243,7 @@
             qs[r, columns] = (query.astype(BF16).astype(F32) * (HD**-0.5)).astype(BF16)
             ks[r, columns] = nt(value, wqkv[1, columns, :]).astype(BF16)
             vs[r, columns] = (nt(value, wqkv[2, columns, :]) + biases[3:4, columns]).astype(BF16)
+            at_steps(i, table)
 
         each(count // LEN, step)
 
@@ -249,7 +253,7 @@
             r, cols = rows_of(s, LEN), rows_of(p, 128)
             q2, k2, v2 = qs[r, cols], ks[r, cols], vs[r, cols]
             results = []
-            kept = stats[r, :]
+            kept = hid[r, :128]
             for part_of in range(2):
                 mine = first if part_of == 0 else ~first
                 scores = nt(jnp.where(mine, q2, jnp.zeros_like(q2)), k2) + bias[s]
@@ -258,7 +262,7 @@
                 total = jnp.sum(expo, axis=-1, keepdims=True)
                 results.append(nn(expo.astype(BF16), v2) * (1.0 / total))
                 kept = jnp.where(lane == 2 * p + part_of, top + jnp.log(total), kept)
-            stats[r, :] = kept
+            hid[r, :128] = kept
             attended[r, cols] = jnp.where(first, results[0], results[1]).astype(BF16)
             at_steps(i, table)
 
@@ -267,30 +271,40 @@
     def run(function, *args):
         return functools.partial(function, *args)
 
-    ag_near(0)
-    project(y)
+    def near(t):
+        return [run(ag_side, t), run(ag_level, t)]
+
+    for t in (q_in, k_in, v_in):
+        ag_near(t)
+    project(y, {0: [run(ag_y, q_in)]})
     attend(
         y,
         {
-            0: [run(ag_y, 0), run(ag_y, 1)],
-            3: [run(ag_level, 0), run(ag_side, 0)],
-            4: [run(ag_side, 1), run(ag_level, 1)],
-            5: [run(ag_y, 2)],
+            0: [run(ag_y, k_in)],
+            1: [*near(q_in), run(ag_y, v_in)],
+            4: near(k_in),
+            5: [run(ag_diag, q_in), *near(v_in), run(ag_y, ups[0]), run(ag_y, downs[0]), run(ag_y, o_in)],
         },
     )
-    ag_diag(0)
-    ag_rest(0)
-    project(1 - y)
+    ag_diag(k_in)
+    ag_diag(v_in)
+    for t in (q_in, k_in, v_in):
+        ag_rest(t)
+    project(1 - y, {1: near(ups[0])})
     attend(
         1 - y,
         {
-            0: [run(ag_diag, 1), run(ag_y, 3)],
-            2: [run(ag_side, 2), run(ag_level, 2)],
-            5: [run(ag_side, 3), run(ag_level, 3), run(ag_diag, 2)],
+            1: [*near(downs[0]), run(ag_y, ups[1])],
+            2: [*near(o_in), run(ag_y, downs[1])],
+            3: [run(ag_diag, ups[0])],
+            5: [run(ag_diag, downs[0]), *near(ups[1]), run(ag_y, ups[2]), run(ag_y, downs[2])],
         },
     )
-    ag_near(1)
-    ag_rest(1)
+    for s in range(sequences):
+        stat_rows[s] = hid[rows_of(s, LEN), :128].T
+    ag_near(o_in)
+    ag_diag(o_in)
+    ag_rest(o_in)
 
     def out_step(i):
         r = rows_of(i, TILE)
@@ -299,21 +313,21 @@
         pltpu.make_async_copy(hid.at[r, :], hidden_hbm.at[r, :], tile_a.at[i]).start()
         normal, _ = normal_of(value)
         n2[r, :] = (normal * vec_recv[0, 5:6, :] + vec_recv[0, 6:7, :]).astype(BF16)
+        at_steps(i, {1: near(downs[1]), 3: [run(ag_diag, ups[1])]})
 
     each(count // TILE, out_step)
-    ag_near(2)
-    ag_rest(2)
-    ag_diag(3)
-    ag_near(3)
-    ag_rest(3)
+    for t in range(o_in + 1, tensors):
+        ag_near(t)
+    ag_rest(ups[0])
+    ag_rest(downs[0])
     pltpu.make_async_copy(cot_hbm, cot, local.at[2]).wait()
 
     up_bias = vec_recv.at[0]
     feed_slots = 2
 
-    def unit(u, kept, cr, yr, xr, zr, er):
+    def unit(u, kept, cr, yr, xr):
         rows = kept.shape[0]
-        return (u, rows, kept, cr, yr, xr, zr, er)
+        return (u, rows, kept, cr, yr, xr)
 
     def own_half(rows):
         return ds(xb * (rows // 2), rows // 2, rows // 4)
@@ -331,52 +345,54 @@
         remote(source, target, unit_send.at[u, k], unit_recv.at[u, k], device).start()
 
     def take_sum(unit_of):
-        u, rows, kept, cr, yr, xr, zr, er = unit_of
+        u, rows, kept, cr, yr, xr = unit_of
         got(cr, unit_recv.at[u, 2])
         got(yr, unit_recv.at[u, 1])
         add_into(kept, cr, yr)
+        pl.semaphore_signal(ready.at[u, 2], inc=1, device_id=level, device_id_type=MESH)
         send_unit(u, 3, kept.at[other_half(rows), :], xr, side)
 
     def far_room(unit_of, i):
-        u, rows, kept, cr, yr, xr, zr, er = unit_of
-        return er if i == 0 else cr.at[(i - 1) * (rows // 4) : i * (rows // 4), :]
+        u, rows, kept, cr, yr, xr = unit_of
+        return cr.at[i * (rows // 4) : (i + 1) * (rows // 4), :]
 
     def send_far(unit_of, i):
-        u, rows, kept, cr, yr, xr, zr, er = unit_of
-        if i > 0:
-            pl.semaphore_wait(ready.at[u, 2 + i], 1)
+        u, rows, kept, cr, yr, xr = unit_of
+        pl.semaphore_wait(ready.at[u, 3 + i], 1)
         send_unit(u, 7 + i, kept.at[own_quarter(rows), :], far_room(unit_of, i), far[i])
 
     def take_side(unit_of):
-        u, rows, kept, cr, yr, xr, zr, er = unit_of
-        for i in range(1, len(far)):
-            pl.semaphore_signal(ready.at[u, 2 + i], inc=1, device_id=far[i], device_id_type=MESH)
+        u, rows, kept, cr, yr, xr = unit_of
+        for i in range(len(far)):
+            pl.semaphore_signal(ready.at[u, 3 + i], inc=1, device_id=far[i], device_id_type=MESH)
         got(xr, unit_recv.at[u, 3])
         sent(xr, unit_send.at[u, 3])
         pl.semaphore_signal(ready.at[u, 0], inc=1, device_id=side, device_id_type=MESH)
         add_into(kept.at[own_half(rows), :], xr)
-        send_unit(u, 4, kept.at[other_quarter(rows), :], zr, level)
+        pl.semaphore_wait(ready.at[u, 2], 1)
+        send_unit(u, 4, kept.at[other_quarter(rows), :], yr.at[: rows // 4, :], level)
 
     def give_level(unit_of):
-        u, rows, kept, cr, yr, xr, zr, er = unit_of
+        u, rows, kept, cr, yr, xr = unit_of
         mine = kept.at[own_quarter(rows), :]
         pl.semaphore_wait(ready.at[u, 1], 1)
         send_unit(u, 5, mine, mine, level)
 
     def take_level(unit_of):
-        u, rows, kept, cr, yr, xr, zr, er = unit_of
-        got(zr, unit_recv.at[u, 4])
-        sent(zr, unit_send.at[u, 4])
+        u, rows, kept, cr, yr, xr = unit_of
+        landed = yr.at[: rows // 4, :]
+        got(landed, unit_recv.at[u, 4])
+        sent(landed, unit_send.at[u, 4])
         pl.semaphore_signal(ready.at[u, 1], inc=1, device_id=level, device_id_type=MESH)
         mine = kept.at[own_quarter(rows), :]
-        add_into(mine, zr)
+        add_into(mine, landed)
         if far:
             send_far(unit_of, 0)
         else:
             give_level(unit_of)
 
     def take_far(unit_of):
-        u, rows, kept, cr, yr, xr, zr, er = unit_of
+        u, rows, kept, cr, yr, xr = unit_of
         mine = kept.at[own_quarter(rows), :]
         for i, _ in enumerate(far):
             landed = far_room(unit_of, i)
@@ -389,28 +405,30 @@
             give_level(unit_of)
 
     def give_side(unit_of):
-        u, rows, kept, cr, yr, xr, zr, er = unit_of
+        u, rows, kept, cr, yr, xr = unit_of
         got(kept.at[other_quarter(rows), :], unit_recv.at[u, 5])
         mine = kept.at[own_half(rows), :]
         pl.semaphore_wait(ready.at[u, 0], 1)
         send_unit(u, 6, mine, mine, side)
 
     def finish(unit_of, target, sem):
-        u, rows, kept, cr, yr, xr, zr, er = unit_of
+        u, rows, kept, cr, yr, xr = unit_of
         got(kept.at[other_half(rows), :], unit_recv.at[u, 6])
         pltpu.make_async_copy(kept, target, sem).start()
 
     def unit_sends(unit_of):
-        u, rows, kept, cr, yr, xr, zr, er = unit_of
+        u, rows, kept, cr, yr, xr = unit_of
         sent(kept, unit_send.at[u, 1])
         sent(kept.at[own_half(rows), :], unit_send.at[u, 6])
         sent(kept.at[own_quarter(rows), :], unit_send.at[u, 5])
 
     feeds = [
-        unit(s, fp.at[feed_slots + 3 + s], fcr.at[s], fyr.at[s], fxr.at[s], fzr.at[s], fer.at[s]) for s in range(3)
+        unit(s, fp.at[feed_slots + 3 + s], fcr.at[s], fyr.at[s], fxr.at[s]) for s in range(3)
     ]
-    proj = unit(3, op.at[3], ocr, oyr, oxr, ozr, oer)
-    attn = unit(4, qp.at[2], qcr, qyr, qxr, qzr, qer)
+    smalls = [
+        unit(3 + n, op.at[4 * n + 3], ocr.at[n], oyr.at[n], oxr.at[n]) for n in range(4)
+    ]
+    proj, heads_a, heads_b, shared = smalls
 
     def feed_first(sub, slot):
         send_unit(sub, 0, fp.at[slot], fcr.at[sub], partner)
@@ -473,7 +491,15 @@
         def _():
             feed_third(sub, slot)
 
-        at_steps(i, {7: [run(take_sum, feeds[0])], 10: [run(take_side, feeds[0])], 11: [run(take_sum, feeds[1])]})
+        at_steps(
+            i,
+            {
+                0: [*near(ups[2]), run(ag_diag, downs[1])],
+                1: [*near(downs[2]), run(ag_rest, ups[1]), run(ag_rest, downs[1])],
+                3: [run(ag_diag, ups[2]), run(ag_diag, downs[2]), run(ag_rest, ups[2]), run(ag_rest, downs[2])],
+                8: [run(take_sum, feeds[0])],
+            },
+        )
 
     vec[8:16, :] = jnp.zeros_like(vec[8:16, :])
     each(steps, feed_step)
@@ -499,34 +525,32 @@
         narrow = grad.astype(BF16)
         gup[r, 3 * width :] = narrow
         n2[r, :] = nt(narrow, w_out[...]).astype(BF16)
-        at_steps(i, {0: [run(take_level, feeds[0])], 3: [run(take_far, feeds[0]), run(take_side, feeds[1])]})
+        at_steps(i, {0: [run(take_side, feeds[0])], 1: [run(take_sum, feeds[1])], 3: [run(take_level, feeds[0])]})
 
     each(count // TILE, hidden_step)
     product = tn(attended[...], gup[:, 3 * width :])
     for m in range(4):
         slot = 2 * jnp.where(y == m // 2, 1, 0) + jnp.where(c == m % 2, 1, 0)
         op[slot] = product[m * part : (m + 1) * part, :].astype(BF16)
-    send_unit(3, 0, op.at[0], ocr, partner)
-
-    def proj_second():
-        got(ocr, unit_recv.at[3, 0])
-        add_into(op.at[1], ocr)
+
+    def small_first(n):
+        send_unit(3 + n, 0, op.at[4 * n], ocr.at[n], partner)
+
+    def small_second(n):
+        got(ocr.at[n], unit_recv.at[3 + n, 0])
+        add_into(op.at[4 * n + 1], ocr.at[n])
         pl.semaphore_signal(credit, inc=1, device_id=partner, device_id_type=MESH)
-        send_unit(3, 1, op.at[1], oyr, above)
-
-    def proj_third():
+        send_unit(3 + n, 1, op.at[4 * n + 1], oyr.at[n], above)
+
+    def small_third(n):
         pl.semaphore_wait(credit, 1)
-        send_unit(3, 2, op.at[2], ocr, partner)
-
+        send_unit(3 + n, 2, op.at[4 * n + 2], ocr.at[n], partner)
+
+    small_first(0)
     def attend_back(side_of, table):
         def step(i):
-            s, p = i // pairs, side_of * pairs + i % pairs
+            s, p = i % sequences, side_of * pairs + 2 * (i // sequences) % pairs
             r, cols = rows_of(s, LEN), rows_of(p, 128)
-
-            @pl.when(i % pairs == 0)
-            def _():
-                stat_rows[...] = stats[r, :].T
-
             q2, k2, v2, d2 = qs[r, cols], ks[r, cols], vs[r, cols], n2[r, cols]
             rq, rk, rv = 0.0, 0.0, 0.0
             for part_of in range(2):
@@ -534,7 +558,7 @@
                 qm = jnp.where(mine, q2, jnp.zeros_like(q2))
                 km = jnp.where(mine, k2, jnp.zeros_like(k2))
                 dm = jnp.where(mine, d2, jnp.zeros_like(d2))
-                probs = jnp.exp(nt(k2, qm) + bias[s] - stat_rows[pl.ds(2 * p + part_of, 1), :])
+                probs = jnp.exp(nt(k2, qm) + bias[s] - stat_rows[s, pl.ds(2 * p + part_of, 1), :])
                 grad_probs = nt(v2, dm)
                 inner = jnp.sum(probs * grad_probs, axis=0, keepdims=True)
                 grad_scores = (probs * (grad_probs - inner)).astype(BF16)
@@ -548,47 +572,57 @@
 
         each(sequences * pairs, step)
 
-    def weight_of_half(side_of, kept_slot):
-        for k in range(3):
-            grads = gup[:, ds(k * width + side_of * half, half, 128)]
-            product = tn(grads, normed[...]).astype(BF16)
-            for core in range(2):
-                slot = jnp.where(c == core, kept_slot, 0)
-                qp[slot, k * part : (k + 1) * part, :] = product[core * part : (core + 1) * part, :]
+    def weight_of_pair(side_of, p):
+        first_column = side_of * half + p * 128
+        grads = jnp.concatenate([gup[:, ds(k * width + first_column, 128)] for k in range(3)], axis=1)
+        return tn(grads, normed[...]).astype(BF16)
+
+    def slot_of(core, late):
+        return jnp.where(c == core, 1, 0) + 2 * late
+
+    def weight_of_outer(side_of, late):
+        for core, p in ((0, 0), (1, 2)):
+            product = weight_of_pair(side_of, p)
+            slot = slot_of(core, late)
+            op[4 + slot] = product[:part]
+            op[8 + slot] = product[part:]
+
+    def weight_of_shared(side_of, late):
+        product = weight_of_pair(side_of, 1)
+        for core in range(2):
+            slot = slot_of(core, late)
+            for k in range(3):
+                start = k * 128 + core * HD
+                op[12 + slot, k * HD : (k + 1) * HD, :] = product[start : start + HD]
 
     attend_back(
         1 - y,
         {
-            0: [proj_second, run(give_side, feeds[0]), run(take_level, feeds[1])],
-            1: [proj_third, run(take_sum, feeds[2])],
-            3: [run(finish, feeds[0], feed_out.at[0], local.at[3]), run(take_far, feeds[1]), run(take_sum, proj)],
-            4: [run(take_side, feeds[2])],
-            5: [run(give_side, feeds[1]), run(take_side, proj)],
+            0: [run(small_second, 0), run(small_third, 0)],
+            1: [run(take_side, feeds[1])],
+            3: [
+                run(weight_of_outer, 1 - y, 0), run(small_first, 1), run(small_first, 2), run(take_sum, feeds[2]),
+                run(take_far, feeds[0]), run(take_level, feeds[1]),
+            ],
+            4: [run(small_second, 1), run(small_second, 2)],
+            5: [run(take_sum, proj)],
         },
     )
-    weight_of_half(1 - y, 1)
-    send_unit(4, 0, qp.at[0], qcr, partner)
-
-    def attn_second():
-        got(qcr, unit_recv.at[4, 0])
-        add_into(qp.at[1], qcr)
-        pl.semaphore_signal(credit, inc=1, device_id=partner, device_id_type=MESH)
-        send_unit(4, 1, qp.at[1], qyr, above)
-
+    weight_of_shared(1 - y, 0)
+    small_first(3)
+    give_side(feeds[0])
     attend_back(
         y,
         {
-            0: [attn_second, run(take_level, feeds[2])],
-            1: [run(take_level, proj)],
-            2: [run(take_far, feeds[2])],
-            3: [run(finish, feeds[1], feed_out.at[1], local.at[4]), run(take_far, proj), run(give_side, feeds[2])],
-            5: [run(give_side, proj), run(finish, feeds[2], feed_out.at[2], local.at[5])],
+            0: [run(small_second, 3)],
+            2: [run(take_side, feeds[2]), run(take_far, feeds[1])],
+            3: [run(weight_of_outer, y, 1), run(small_third, 1), run(small_third, 2), run(take_side, proj)],
+            5: [run(take_sum, heads_a), run(take_sum, heads_b), run(give_side, feeds[1])],
         },
     )
-    sent(qp.at[0], unit_send.at[4, 0])
-    weight_of_half(y, 2)
-    pl.semaphore_wait(credit, 1)
-    send_unit(4, 2, qp.at[0], qcr, partner)
+    weight_of_shared(y, 1)
+    small_third(3)
+    finish(feeds[0], feed_out.at[0], local.at[3])
 
     def input_step(i):
         r = rows_of(i, TILE)
@@ -602,7 +636,14 @@
         vec[3:4, :] += column_sum(v.astype(F32))
         pltpu.make_async_copy(hid.at[r, :], grad_x.at[r, :], tile_a.at[i]).start()
         pltpu.make_async_copy(act_hbm.at[r, :], gup.at[r, :], tile_b.at[i]).start()
-        at_steps(i, {0: [run(take_sum, attn)], 3: [run(finish, proj, proj_out, local.at[6])]})
+        at_steps(
+            i,
+            {
+                0: [run(take_level, feeds[2])],
+                1: [run(take_sum, shared), run(take_level, proj)],
+                2: [run(take_side, heads_a)],
+            },
+        )
 
     each(count // TILE, input_step)
 
@@ -640,32 +681,68 @@
         at_steps(
             i,
             {
-                0: [run(vec_step, 0)],
+                0: [run(take_side, heads_b), run(vec_step, 0)],
                 1: [run(vec_step, 1)],
-                2: [run(take_side, attn), run(vec_step, 2)],
-                3: [run(vec_step, 3)],
+                2: [run(take_level, heads_a), run(vec_step, 2)],
+                3: [run(take_level, heads_b), run(take_far, feeds[2]), run(vec_step, 3)],
             },
         )
 
     each(count // TILE, output_step)
-    take_level(attn)
     for i in range(4, len(rounds)):
         vec_step(i)
     pltpu.make_async_copy(vec, vec_out, local.at[7]).start()
-    take_far(attn)
-    give_side(attn)
-    finish(attn, qkv_out, local.at[8])
+
+    def place(n):
+        kept = smalls[n][2]
+        pair_at, shared_at = HD * c, 2 * HD * (1 - c)
+        if n == 1:
+            moves = ((0, 128, pair_at), (128, 64, part + pair_at))
+        elif n == 2:
+            moves = ((0, 64, part + pair_at + 64), (64, 128, 2 * part + pair_at))
+        else:
+            moves = tuple((k * HD, HD, k * part + shared_at) for k in range(3))
+        return [
+            pltpu.make_async_copy(
+                kept.at[start : start + rows, :], qkv_out.at[ds(where, rows, HD), :], local.at[6 + 2 * n + k]
+            )
+            for k, (start, rows, where) in enumerate(moves)
+        ]
+
+    def finish_heads(n):
+        rows = smalls[n][1]
+        got(smalls[n][2].at[other_half(rows), :], unit_recv.at[3 + n, 6])
+        for copy in place(n):
+            copy.start()
+
+    finish(feeds[1], feed_out.at[1], local.at[4])
+    take_far(proj)
+    take_side(shared)
+    take_far(heads_a)
+    take_far(heads_b)
+    give_side(feeds[2])
+    give_side(proj)
+    take_level(shared)
+    give_side(heads_a)
+    give_side(heads_b)
+    take_far(shared)
+    finish(feeds[2], feed_out.at[2], local.at[5])
+    give_side(shared)
+    finish(proj, proj_out, local.at[6])
+    finish_heads(1)
+    finish_heads(2)
+    finish_heads(3)
 
     for i in range(3):
         sent(small_own, small_send.at[i])
-    for t in range(4):
+    for t in range(tensors):
         ag_sends(t)
     for k, slot in ((1, 0), (2, 1)):
         sent(fp.at[slot], unit_send.at[k, 2])
-    for k in (0, 2):
-        sent(op.at[0], unit_send.at[3, k])
-    sent(qp.at[0], unit_send.at[4, 2])
-    for unit_of in feeds + [proj, attn]:
+    for n in range(4):
+        for k in (0, 2):
+            sent(op.at[4 * n + k], unit_send.at[3 + n, k])
+    for unit_of in feeds + smalls:
         unit_sends(unit_of)
     for i in range(count // TILE):
         r = rows_of(i, TILE)
@@ -673,8 +750,10 @@
     for s in range(3):
         pltpu.make_async_copy(feeds[s][2], feed_out.at[s], local.at[3 + s]).wait()
     pltpu.make_async_copy(op.at[3], proj_out, local.at[6]).wait()
+    for n in range(1, 4):
+        for copy in place(n):
+            copy.wait()
     pltpu.make_async_copy(vec, vec_out, local.at[7]).wait()
-    pltpu.make_async_copy(qp.at[2], qkv_out, local.at[8]).wait()
 
 
 def per_device(
@@ -700,6 +779,7 @@
         return pltpu.VMEM(dims, kind)
 
     unit_rows = 2 * PIECE
+    tensors = 4 + 2 * (feed // PIECE)
     dma = pltpu.SemaphoreType.DMA
     outs = [
         shape(count, width), shape(count, width, kind=F32), shape(3, unit_rows, width), shape(part, width),
@@ -709,19 +789,19 @@
     def unit_rooms(rows, slots, lead):
         return [
             room(slots, rows, width), room(*lead, rows, width), room(*lead, rows, width),
-            room(*lead, rows // 2, width), room(*lead, rows // 4, width), room(*lead, rows // 4, width),
+            room(*lead, rows // 2, width),
         ]
 
     scratch = [
         room(mp, 16, width), room(3, width, width), room(width, width), room(mp, width, feed), room(mp, feed, width),
         *[room(count, width) for _ in range(8)],
-        room(count, 128, kind=F32), room(count, width, kind=F32), room(count, mp * feed), room(2, count, PIECE),
-        room(count // LEN, LEN, LEN, kind=F32), room(128, LEN, kind=F32), room(16, width, kind=F32),
+        room(count, width, kind=F32), room(count, mp * feed), room(2, count, PIECE),
+        room(count // LEN, LEN, LEN, kind=F32), room(count // LEN, 128, LEN, kind=F32), room(16, width, kind=F32),
         room(1 + 2 + bits, 16, width, kind=F32),
-        *unit_rooms(unit_rows, 8, (3,)), *unit_rooms(part, 4, ()), *unit_rooms(3 * part, 3, ()),
-        dma((4,)), dma((4, 9)), dma((4, 9)), dma((3,)), dma((3,)), dma((9,)), dma((2,)), dma((4,)), dma((4,)),
-        dma((5, 7 + max(far, 1))), dma((5, 7 + max(far, 1))), dma((2 + bits,)), dma((2 + bits,)),
-        pltpu.SemaphoreType.REGULAR, pltpu.SemaphoreType.REGULAR((5, 2 + max(far, 1))),
+        *unit_rooms(unit_rows, 8, (3,)), *unit_rooms(part, 16, (4,)),
+        dma((tensors,)), dma((tensors, 9)), dma((tensors, 9)), dma((3,)), dma((3,)), dma((15,)), dma((2,)), dma((4,)), dma((4,)),
+        dma((7, 7 + max(far, 1))), dma((7, 7 + max(far, 1))), dma((2 + bits,)), dma((2 + bits,)),
+        pltpu.SemaphoreType.REGULAR, pltpu.SemaphoreType.REGULAR((7, 3 + max(far, 1))),
     ]
     args = (
         small_own, qkv_own, w_out, w_up, w_down, tokens, cotangent, segment.reshape(-1, LEN),

time: 248 us -> 210 us (0.85)
  Pallas kernels: 222 us -> 184 us
    pallas_call x1, Pallas kernels: 222 us -> 184 us  [per_device(): pl.pallas_call(functools.partial(layer_kernel, dp), out_shape=outs, in_sp...]
where the time goes in v3:
time: 210 us
  Pallas kernels  184 us (88%)
  local copies, waits for them, and re-layouts  21 us (10%)
  other arithmetic  4.12 us (2%)
    pallas_call x1, Pallas kernels, per_device(): pl.pallas_call(functools.partial(layer_kernel, dp), out_shape=outs, in_sp...  184 us
    another operation x7, local copies, waits for them, and re-layouts, per_device(): jnp.stack([ln1_gain, ln1_bias, b_qv[0], b_qv[1], b_out, ln2_gain, ln2_bia...  4.65 us

profile of v3, /device:TPU:0, one launch (start us, length us, event | category | flops | bytes accessed | tf_op | source)
XLA Modules:
  0.0 209.6 jit_solution(11896755333747347706)
XLA Ops:
  0.7 0.7 stack.22
  1.3 0.7 stack.23
  2.0 0.7 stack.24
  2.6 0.7 stack.25
  3.3 0.7 stack.26
  3.9 0.7 stack.27
  4.6 0.7 stack.28
  5.3 0.6 broadcast_in_dim.3
  5.9 2.6 %dynamic_update_slice.6 = bf16[16,768]{1,0:T(8,128)(2,1)} dynamic-update-slice(bf16[16,768]{1,0:T(8,128)(2,1)} %broadcast_in_dim.3, bf16[8,192]{1,0:T(8,128)(2,1)S(1)} %stack.28, s32[]{:T(128)} %constant.2.clone.1, s32[]{:T(128)S(6)} %select_n.8) | dynamic-update-slice | bytes 6148 | tf_op jit(solution)/shard_map/dynamic_update_slice | solution.py:771
  8.5 0.7 reshape.46
  9.2 1.3 dynamic_update_slice.7.small_own
  10.5 1.3 reshape.47.segment
  11.8 183.8 %shard_map.254 = (bf16[1024,768]{1,0:T(8,128)(2,1)}, f32[1024,768]{1,0:T(8,128)}, bf16[3,512,768]{2,1,0:T(8,128)(2,1)}, bf16[192,768]{1,0:T(8,128)(2,1)}, bf16[5...) custom-call(bf16[16,768]{1,0:T(8,128)(2,1)} %dynamic_update_slice.7.small_own, ...), custom_call_target="tpu_custom_call" | custom-call | tf_op jit(solution)/shard_map/pallas_call | solution.py:809
  195.7 1.8 fusion
  197.5 1.9 bitcast_convert_fusion
  199.4 0.0 copy-start.4
  199.4 0.0 copy-start.2
  199.4 1.9 copy.29
  201.4 0.0 copy-start.3
  201.4 0.0 copy-done.4
  201.4 0.7 fusion.1
  202.0 0.7 dynamic-slice.2
  202.7 0.6 dynamic-slice_reduce_fusion
  203.3 0.0 copy-done.2
  203.3 0.0 copy-start.1
  203.3 1.4 convert_bitcast_fusion
  204.7 0.0 copy-done.3
  204.7 0.9 convert_element_type.30
  205.5 0.0 copy-done.1
  205.5 1.1 copy.34
  206.7 1.3 copy-done
  208.0 1.7 copy.35
  (2 shorter events, 0.0 us)
Async XLA Ops:
  199.4 2.0 copy-start.4
  199.4 3.9 %copy-start.2 = (bf16[576,768]{1,0:T(8,128)(2,1)S(1)}, bf16[576,768]{1,0:T(8,128)(2,1)}, u32[]{:S(2)}) copy-start(bf16[576,768]{1,0:T(8,128)(2,1)} %get-tuple-element.23) | copy-start | bytes 2654212
  201.4 3.3 %copy-start.3 = (bf16[192,768]{1,0:T(8,128)(2,1)S(1)}, bf16[192,768]{1,0:T(8,128)(2,1)}, u32[]{:S(2)}) copy-start(bf16[192,768]{1,0:T(8,128)(2,1)} %get-tuple-element.24) | copy-start | bytes 884740
  203.3 2.2 %copy-start.1 = (bf16[1024,768]{1,0:T(8,128)(2,1)S(1)}, bf16[1024,768]{1,0:T(8,128)(2,1)}, u32[]{:S(2)}) copy-start(bf16[1024,768]{1,0:T(8,128)(2,1)} %get-tuple-element.50) | copy-start | bytes 4718596
  205.5 2.5 %copy-start = (f32[1024,768]{1,0:T(8,128)S(1)}, f32[1024,768]{1,0:T(8,128)}, u32[]{:S(2)}) copy-start(f32[1024,768]{1,0:T(8,128)} %get-tuple-element.51) | copy-start | bytes 9437188

commit v4 on v3

--- a/solution.py
+++ b/solution.py
@@ -86,10 +86,10 @@
 
 def layer_kernel(
     dp, small_own, qkv_own, out_own, up_own, down_own, tokens, cot_hbm, segment,
-    output, grad_x, feed_out, proj_out, qkv_out, vec_out, act_hbm, hidden_hbm,
+    output, grad_x, down_out, up_out, proj_out, qkv_out, vec_out, act_hbm, hidden_hbm,
     small, wqkv, w_out, w_up, w_down, x, cot, normed, qs, ks, vs, attended, n2, hid, gup, act, bias,
     stat_rows, vec, vec_recv, fp, fcr, fyr, fxr, op, ocr, oyr, oxr,
-    ag_local, ag_send, ag_recv, small_send, small_recv, local, act_sem, tile_a, tile_b, unit_send, unit_recv,
+    ag_local, ag_send, ag_recv, small_send, small_recv, local, feed_done, act_sem, tile_a, tile_b, tile_c, unit_send, unit_recv,
     vec_send, vec_got, credit, ready,
 ):
     me, d = lax.axis_index("mp"), lax.axis_index("dp")
@@ -216,7 +216,15 @@
     pltpu.make_async_copy(small_own, small.at[me], local.at[0]).wait()
     for i, m in enumerate((m_diag, m_y, m_core)):
         got(small.at[m], small_recv.at[i])
-    vectors = sum(small[m].astype(F32) for m in range(4))
+    place_row = lax.broadcasted_iota(jnp.int32, (part, width), 0)
+    place_column = lax.broadcasted_iota(jnp.int32, (part, width), 1)
+    vec_recv[0] = jnp.zeros(vec_recv.shape[1:], F32)
+    for m in range(4):
+        into = jnp.where(place_column == place_row + m * part, 1.0, 0.0).astype(BF16)
+        vec_recv[0, :8, :] += nn(small[m, :8, :], into)
+        for owner in range(4):
+            vec_recv[0, 8 + owner : 9 + owner, :] += nn(small[owner, 8 + m : 9 + m, :], into)
+    vectors = vec_recv[0]
     pltpu.make_async_copy(tokens.at[ds(0, count), :], x, local.at[1]).wait()
     g1, b1, b_query, b_value, b_out, g2, b2, b_down = (vectors[i : i + 1] for i in range(8))
 
@@ -229,8 +237,6 @@
     lane = lax.broadcasted_iota(jnp.int32, (LEN, 128), 1)
     first = lane < HD
     pairs = half // 128
-    small_sum = sum(small[m].astype(F32) for m in range(4))
-    vec_recv[0] = small_sum
 
     def project(side_of, table):
         columns = ds(side_of * half, half, 128)
@@ -324,6 +330,7 @@
 
     up_bias = vec_recv.at[0]
     feed_slots = 2
+    rounds_far = max(len(far), 1)
 
     def unit(u, kept, cr, yr, xr):
         rows = kept.shape[0]
@@ -377,6 +384,8 @@
         mine = kept.at[own_quarter(rows), :]
         pl.semaphore_wait(ready.at[u, 1], 1)
         send_unit(u, 5, mine, mine, level)
+        pl.semaphore_wait(ready.at[u, 0], 1)
+        send_unit(u, 6, mine, mine, side)
 
     def take_level(unit_of):
         u, rows, kept, cr, yr, xr = unit_of
@@ -406,21 +415,32 @@
 
     def give_side(unit_of):
         u, rows, kept, cr, yr, xr = unit_of
-        got(kept.at[other_quarter(rows), :], unit_recv.at[u, 5])
-        mine = kept.at[own_half(rows), :]
-        pl.semaphore_wait(ready.at[u, 0], 1)
-        send_unit(u, 6, mine, mine, side)
-
-    def finish(unit_of, target, sem):
-        u, rows, kept, cr, yr, xr = unit_of
-        got(kept.at[other_half(rows), :], unit_recv.at[u, 6])
-        pltpu.make_async_copy(kept, target, sem).start()
+        other = kept.at[other_quarter(rows), :]
+        got(other, unit_recv.at[u, 5])
+        send_unit(u, 7 + rounds_far, other, other, side)
+
+    def finish(unit_of, copies):
+        u, rows, kept, cr, yr, xr = unit_of
+        got(kept.at[own_quarter(rows), :], unit_recv.at[u, 6])
+        got(kept.at[own_quarter(rows), :], unit_recv.at[u, 7 + rounds_far])
+        for copy in copies():
+            copy.start()
+
+    def place_feed(sub):
+        kept, piece = feeds[sub][2], slice(sub * PIECE, (sub + 1) * PIECE)
+        blocks = [slice(k * PIECE, (k + 1) * PIECE) for k in range(width // PIECE)]
+        moves = [(kept.at[:PIECE, :], down_out.at[piece, :])]
+        moves += [(kept.at[PIECE:, block], up_out.at[block, piece]) for block in blocks]
+        return [pltpu.make_async_copy(*move, feed_done.at[sub, k]) for k, move in enumerate(moves)]
+
+    def place_proj():
+        return [pltpu.make_async_copy(op.at[3], proj_out, local.at[6])]
 
     def unit_sends(unit_of):
         u, rows, kept, cr, yr, xr = unit_of
-        sent(kept, unit_send.at[u, 1])
-        sent(kept.at[own_half(rows), :], unit_send.at[u, 6])
-        sent(kept.at[own_quarter(rows), :], unit_send.at[u, 5])
+        sent(kept.at[own_half(rows), :] if u == 2 else kept, unit_send.at[u, 1])
+        for k in (5, 6, 7 + rounds_far):
+            sent(kept.at[own_quarter(rows), :], unit_send.at[u, k])
 
     feeds = [
         unit(s, fp.at[feed_slots + 3 + s], fcr.at[s], fyr.at[s], fxr.at[s]) for s in range(3)
@@ -437,7 +457,43 @@
         got(fcr.at[sub], unit_recv.at[sub, 0])
         add_into(fp.at[slot], fcr.at[sub])
         pl.semaphore_signal(credit, inc=1, device_id=partner, device_id_type=MESH)
-        send_unit(sub, 1, fp.at[slot], fyr.at[sub], above)
+
+        @pl.when(sub < 2)
+        def _():
+            send_unit(sub, 1, fp.at[slot], fyr.at[sub], above)
+
+        @pl.when(sub == 2)
+        def _():
+            rows = fp.shape[1]
+            send_unit(2, 8 + rounds_far, fp.at[slot, other_half(rows), :], fyr.at[2, own_half(rows), :], side)
+
+    def last_other():
+        _, rows, _, _, yr, _ = feeds[2]
+        passed = fp.at[feed_slots + 2]
+        landed = yr.at[other_half(rows), :]
+        got(landed, unit_recv.at[2, 8 + rounds_far])
+        add_into(passed.at[own_half(rows), :], landed)
+        send_unit(2, 1, passed.at[own_half(rows), :], yr.at[own_half(rows), :], above)
+
+    def last_sum():
+        u, rows, kept, cr, _, xr = feeds[2]
+        got(cr, unit_recv.at[u, 2])
+        add_into(kept, cr)
+        for i in range(len(far)):
+            pl.semaphore_signal(ready.at[u, 3 + i], inc=1, device_id=far[i], device_id_type=MESH)
+        send_unit(u, 3, kept.at[other_half(rows), :], xr, side)
+
+    def last_both():
+        u, rows, kept, _, yr, xr = feeds[2]
+        mine, landed = kept.at[own_half(rows), :], yr.at[own_half(rows), :]
+        got(xr, unit_recv.at[u, 3])
+        sent(xr, unit_send.at[u, 3])
+        pl.semaphore_signal(ready.at[u, 0], inc=1, device_id=side, device_id_type=MESH)
+        got(landed, unit_recv.at[u, 1])
+        add_into(mine, xr, landed)
+        pl.semaphore_signal(ready.at[u, 2], inc=1, device_id=level, device_id_type=MESH)
+        pl.semaphore_wait(ready.at[u, 2], 1)
+        send_unit(u, 4, kept.at[other_quarter(rows), :], yr.at[: rows // 4, :], level)
 
     def feed_third(sub, slot):
         pl.semaphore_wait(credit, 1)
@@ -477,7 +533,9 @@
         each(count // LEN, rows_step)
         pltpu.make_async_copy(act.at[buffer], act_hbm.at[:, whole], act_sem.at[buffer]).start()
         fp[slot, :PIECE, :] = tn(act[buffer], cot[...]).astype(BF16)
-        fp[slot, PIECE:, :] = tn(gup[:, whole], n2[...]).astype(BF16)
+        product = tn(n2[...], gup[:, whole]).astype(BF16)
+        for k in range(width // PIECE):
+            fp[slot, PIECE:, k * PIECE : (k + 1) * PIECE] = product[k * PIECE : (k + 1) * PIECE, :]
 
         @pl.when((late == 0) & (odd == 0))
         def _():
@@ -498,6 +556,7 @@
                 1: [*near(downs[2]), run(ag_rest, ups[1]), run(ag_rest, downs[1])],
                 3: [run(ag_diag, ups[2]), run(ag_diag, downs[2]), run(ag_rest, ups[2]), run(ag_rest, downs[2])],
                 8: [run(take_sum, feeds[0])],
+                9: [last_other],
             },
         )
 
@@ -525,7 +584,7 @@
         narrow = grad.astype(BF16)
         gup[r, 3 * width :] = narrow
         n2[r, :] = nt(narrow, w_out[...]).astype(BF16)
-        at_steps(i, {0: [run(take_side, feeds[0])], 1: [run(take_sum, feeds[1])], 3: [run(take_level, feeds[0])]})
+        at_steps(i, {0: [last_sum, run(take_side, feeds[0])], 1: [run(take_sum, feeds[1])], 3: [run(take_level, feeds[0])]})
 
     each(count // TILE, hidden_step)
     product = tn(attended[...], gup[:, 3 * width :])
@@ -598,31 +657,30 @@
     attend_back(
         1 - y,
         {
-            0: [run(small_second, 0), run(small_third, 0)],
-            1: [run(take_side, feeds[1])],
+            0: [run(small_second, 0), run(small_third, 0), last_both],
             3: [
-                run(weight_of_outer, 1 - y, 0), run(small_first, 1), run(small_first, 2), run(take_sum, feeds[2]),
-                run(take_far, feeds[0]), run(take_level, feeds[1]),
+                run(weight_of_outer, 1 - y, 0), run(small_first, 1), run(small_first, 2), run(take_level, feeds[2]),
+                run(take_far, feeds[0]), run(take_side, feeds[1]), run(take_sum, proj),
             ],
             4: [run(small_second, 1), run(small_second, 2)],
-            5: [run(take_sum, proj)],
         },
     )
     weight_of_shared(1 - y, 0)
     small_first(3)
-    give_side(feeds[0])
+    take_side(proj)
     attend_back(
         y,
         {
-            0: [run(small_second, 3)],
-            2: [run(take_side, feeds[2]), run(take_far, feeds[1])],
-            3: [run(weight_of_outer, y, 1), run(small_third, 1), run(small_third, 2), run(take_side, proj)],
-            5: [run(take_sum, heads_a), run(take_sum, heads_b), run(give_side, feeds[1])],
+            0: [run(small_second, 3), run(give_side, feeds[0])],
+            2: [run(take_level, feeds[1])],
+            3: [run(weight_of_outer, y, 1), run(small_third, 1), run(small_third, 2), run(take_far, feeds[2])],
+            4: [run(take_sum, heads_a), run(take_level, proj)],
+            5: [run(take_sum, heads_b)],
         },
     )
     weight_of_shared(y, 1)
     small_third(3)
-    finish(feeds[0], feed_out.at[0], local.at[3])
+    finish(feeds[0], run(place_feed, 0))
 
     def input_step(i):
         r = rows_of(i, TILE)
@@ -634,14 +692,14 @@
         vec[1:2, :] += column_sum(incoming)
         vec[2:3, :] += column_sum(q.astype(F32))
         vec[3:4, :] += column_sum(v.astype(F32))
-        pltpu.make_async_copy(hid.at[r, :], grad_x.at[r, :], tile_a.at[i]).start()
+        pltpu.make_async_copy(hid.at[r, :], grad_x.at[r, :], tile_c.at[i]).start()
         pltpu.make_async_copy(act_hbm.at[r, :], gup.at[r, :], tile_b.at[i]).start()
         at_steps(
             i,
             {
-                0: [run(take_level, feeds[2])],
-                1: [run(take_sum, shared), run(take_level, proj)],
-                2: [run(take_side, heads_a)],
+                0: [run(take_side, heads_a)],
+                1: [run(take_sum, shared), run(take_far, feeds[1]), run(give_side, feeds[2])],
+                3: [run(take_side, heads_b), run(take_far, proj)],
             },
         )
 
@@ -649,7 +707,7 @@
 
     def reload(i):
         r = rows_of(i, TILE)
-        pltpu.make_async_copy(hid.at[r, :], grad_x.at[r, :], tile_a.at[i]).wait()
+        pltpu.make_async_copy(hid.at[r, :], grad_x.at[r, :], tile_c.at[i]).wait()
         pltpu.make_async_copy(hidden_hbm.at[r, :], hid.at[r, :], tile_a.at[i]).start()
 
     each(count // TILE, reload)
@@ -681,18 +739,14 @@
         at_steps(
             i,
             {
-                0: [run(take_side, heads_b), run(vec_step, 0)],
-                1: [run(vec_step, 1)],
-                2: [run(take_level, heads_a), run(vec_step, 2)],
-                3: [run(take_level, heads_b), run(take_far, feeds[2]), run(vec_step, 3)],
+                0: [run(take_level, heads_a), run(vec_step, 0)],
+                1: [run(take_side, shared), run(vec_step, 1)],
+                2: [run(give_side, feeds[1]), run(vec_step, 2)],
+                3: [run(take_level, heads_b), run(vec_step, 3)],
             },
         )
 
     each(count // TILE, output_step)
-    for i in range(4, len(rounds)):
-        vec_step(i)
-    pltpu.make_async_copy(vec, vec_out, local.at[7]).start()
-
     def place(n):
         kept = smalls[n][2]
         pair_at, shared_at = HD * c, 2 * HD * (1 - c)
@@ -709,29 +763,23 @@
             for k, (start, rows, where) in enumerate(moves)
         ]
 
-    def finish_heads(n):
-        rows = smalls[n][1]
-        got(smalls[n][2].at[other_half(rows), :], unit_recv.at[3 + n, 6])
-        for copy in place(n):
-            copy.start()
-
-    finish(feeds[1], feed_out.at[1], local.at[4])
-    take_far(proj)
-    take_side(shared)
+    give_side(proj)
     take_far(heads_a)
+    finish(feeds[2], run(place_feed, 2))
+    take_level(shared)
     take_far(heads_b)
-    give_side(feeds[2])
-    give_side(proj)
-    take_level(shared)
     give_side(heads_a)
+    for i in range(4, len(rounds)):
+        vec_step(i)
+    pltpu.make_async_copy(vec, vec_out, local.at[7]).start()
+    take_far(shared)
     give_side(heads_b)
-    take_far(shared)
-    finish(feeds[2], feed_out.at[2], local.at[5])
+    finish(feeds[1], run(place_feed, 1))
     give_side(shared)
-    finish(proj, proj_out, local.at[6])
-    finish_heads(1)
-    finish_heads(2)
-    finish_heads(3)
+    finish(proj, place_proj)
+    finish(heads_a, run(place, 1))
+    finish(heads_b, run(place, 2))
+    finish(shared, run(place, 3))
 
     for i in range(3):
         sent(small_own, small_send.at[i])
@@ -742,14 +790,16 @@
     for n in range(4):
         for k in (0, 2):
             sent(op.at[4 * n + k], unit_send.at[3 + n, k])
+    sent(feeds[2][2].at[own_half(2 * PIECE), :], unit_send.at[2, 8 + rounds_far])
     for unit_of in feeds + smalls:
         unit_sends(unit_of)
     for i in range(count // TILE):
         r = rows_of(i, TILE)
         pltpu.make_async_copy(x.at[r, :], output.at[r, :], tile_a.at[i]).wait()
     for s in range(3):
-        pltpu.make_async_copy(feeds[s][2], feed_out.at[s], local.at[3 + s]).wait()
-    pltpu.make_async_copy(op.at[3], proj_out, local.at[6]).wait()
+        for copy in place_feed(s):
+            copy.wait()
+    place_proj()[0].wait()
     for n in range(1, 4):
         for copy in place(n):
             copy.wait()
@@ -767,9 +817,12 @@
     feed = w_up.shape[1]
     bits = dp.bit_length() - 1
     far = bits - 2
-    pieces = jnp.stack([ln1_gain, ln1_bias, b_qv[0], b_qv[1], b_out, ln2_gain, ln2_bias, b_down])
-    small_own = lax.dynamic_update_slice(jnp.zeros((16, width), BF16), pieces, (0, me * part))
-    small_own = lax.dynamic_update_slice(small_own, b_up.reshape(1, feed), (8 + me, 0))
+    small_own = jnp.pad(b_up.reshape(-1, part), ((8, 0), (0, 0)))
+    place = lax.broadcasted_iota(jnp.int32, small_own.shape, 0) * part + lax.broadcasted_iota(
+        jnp.int32, small_own.shape, 1
+    )
+    for i, piece in reversed(list(enumerate((ln1_gain, ln1_bias, b_qv[0], b_qv[1], b_out, ln2_gain, ln2_bias, b_down)))):
+        small_own = jnp.where(place < (i + 1) * part, piece[None, :], small_own)
     qkv_own = w_qkv.swapaxes(1, 2)
 
     def shape(*dims, kind=BF16):
@@ -782,7 +835,7 @@
     tensors = 4 + 2 * (feed // PIECE)
     dma = pltpu.SemaphoreType.DMA
     outs = [
-        shape(count, width), shape(count, width, kind=F32), shape(3, unit_rows, width), shape(part, width),
+        shape(count, width), shape(count, width, kind=F32), shape(feed, width), shape(width, feed), shape(part, width),
         shape(3 * part, width), shape(16, width, kind=F32), shape(count, mp * feed), shape(count, width, kind=F32),
     ]
 
@@ -793,14 +846,14 @@
         ]
 
     scratch = [
-        room(mp, 16, width), room(3, width, width), room(width, width), room(mp, width, feed), room(mp, feed, width),
+        room(mp, 8 + mp, part), room(3, width, width), room(width, width), room(mp, width, feed), room(mp, feed, width),
         *[room(count, width) for _ in range(8)],
         room(count, width, kind=F32), room(count, mp * feed), room(2, count, PIECE),
         room(count // LEN, LEN, LEN, kind=F32), room(count // LEN, 128, LEN, kind=F32), room(16, width, kind=F32),
         room(1 + 2 + bits, 16, width, kind=F32),
         *unit_rooms(unit_rows, 8, (3,)), *unit_rooms(part, 16, (4,)),
-        dma((tensors,)), dma((tensors, 9)), dma((tensors, 9)), dma((3,)), dma((3,)), dma((15,)), dma((2,)), dma((4,)), dma((4,)),
-        dma((7, 7 + max(far, 1))), dma((7, 7 + max(far, 1))), dma((2 + bits,)), dma((2 + bits,)),
+        dma((tensors,)), dma((tensors, 9)), dma((tensors, 9)), dma((3,)), dma((3,)), dma((15,)), dma((3, 1 + width // PIECE)), dma((2,)), dma((4,)), dma((4,)), dma((4,)),
+        dma((7, 9 + max(far, 1))), dma((7, 9 + max(far, 1))), dma((2 + bits,)), dma((2 + bits,)),
         pltpu.SemaphoreType.REGULAR, pltpu.SemaphoreType.REGULAR((7, 3 + max(far, 1))),
     ]
     args = (
@@ -816,15 +869,13 @@
             vmem_limit_bytes=VMEM_LIMIT, collective_id=0, has_side_effects=True
         ),
     )(*args)
-    output, grad_x, feeds, proj, attn, vec = results[:6]
+    output, grad_x, g_down, g_up, proj, attn, vec = results[:7]
     eight = lax.dynamic_slice_in_dim(vec[:8], me * part, part, 1)
     grad_b_up = lax.dynamic_slice_in_dim(vec, 8 + me, 1, 0).reshape(-1)
-    g_down = feeds[:, :PIECE].reshape(feed, width).astype(F32)
-    g_up = feeds[:, PIECE:].reshape(feed, width).T.astype(F32)
     g_qkv = attn.reshape(3, part, width).swapaxes(1, 2).astype(F32)
     return (
         output, grad_x, eight[0], eight[1], g_qkv, eight[2:4], proj.astype(F32), eight[4], eight[5], eight[6],
-        g_up, grad_b_up, g_down, eight[7],
+        g_up.astype(F32), grad_b_up, g_down.astype(F32), eight[7],
     )
 
 

time: 210 us -> 194 us (0.924)
  local copies, waits for them, and re-layouts: 21 us -> 10.6 us
  Pallas kernels: 184 us -> 174 us
  other arithmetic: 4.12 us -> 8.04 us
    pallas_call x1, Pallas kernels: 184 us -> 174 us  [per_device(): pl.pallas_call(functools.partial(layer_kernel, dp), out_shape=outs, in_sp...]
    another operation x7 -> x0, local copies, waits for them, and re-layouts: 4.65 us -> none  [per_device(): jnp.stack([ln1_gain, ln1_bias, b_qv[0], b_qv[1], b_out, ln2_gain, ln2_bia...]
    dynamic_update_slice x2 -> x0, local copies, waits for them, and re-layouts: 3.91 us -> none  [the longest x1 2.59 us: per_device(): lax.dynamic_update_slice(jnp.zeros((16, width), BF16), pieces, (0, me * p...]
where the time goes in v4:
time: 194 us; the launch traced here: 193 us
  Pallas kernels  174 us (90%)
  local copies, waits for them, and re-layouts  10.6 us (5%)
  other arithmetic  8.04 us (4%)
    pallas_call x1, Pallas kernels, per_device(): pl.pallas_call(functools.partial(layer_kernel, dp), out_shape=outs, in_sp...  174 us
    unnamed x12, local copies, waits for them, and re-layouts  4.25 us

profile of v4, /device:TPU:0, one launch (start us, length us, event | category | flops | bytes accessed | tf_op | source)
XLA Modules:
  0.0 193.0 jit_solution(7943051523660324919)
XLA Ops:
  0.6 0.8 reshape.46
  1.4 0.8 slice_reduce_fusion.1
  2.2 1.4 fusion.8.small_own
  3.6 1.3 reshape.47.segment
  4.9 173.8 %shard_map.254 = (bf16[1024,768]{1,0:T(8,128)(2,1)}, f32[1024,768]{1,0:T(8,128)}, bf16[768,768]{1,0:T(8,128)(2,1)}, bf16[768,768]{1,0:T(8,128)(2,1)}, bf16[192,7...) custom-call(bf16[12,192]{1,0:T(8,128)(2,1)} %fusion.8.small_own, ...), custom_call_target="tpu_custom_call" | custom-call | tf_op jit(solution)/shard_map/pallas_call | solution.py:862
  178.7 0.0 copy-start.4
  178.7 0.8 slice.32
  179.5 0.7 fusion.16
  180.2 0.0 copy-start.3
  180.2 2.6 %convert_bitcast_fusion = f32[3,768,192]{1,2,0:T(8,128)} fusion(bf16[3,192,768]{2,1,0:T(8,128)(2,1)} %bitcast.12), kind=kLoop, calls=%fused_computation | loop fusion | flops 442368 | bytes 2654208 | tf_op jit(solution)/shard_map/convert_element_type | solution.py:875
  182.8 0.7 dynamic-slice.2
  183.4 0.0 copy-done.4
  183.4 0.9 convert_element_type.23
  184.3 0.0 copy-done.3
  184.3 0.0 copy-start.2
  184.3 1.6 convert_element_type.24
  185.9 1.3 dynamic-slice_reduce_fusion
  187.2 0.0 copy-done.2
  187.2 0.0 copy-start.1
  187.2 1.6 convert_element_type.25
  188.8 0.0 copy-start
  188.8 0.5 copy-done.1
  189.3 1.1 copy.31
  190.5 0.9 copy-done
  191.4 1.7 copy.32
  (1 shorter events, 0.0 us)
Async XLA Ops:
  178.7 4.7 %copy-start.4 = (bf16[192,768]{1,0:T(8,128)(2,1)S(1)}, bf16[192,768]{1,0:T(8,128)(2,1)}, u32[]{:S(2)}) copy-start(bf16[192,768]{1,0:T(8,128)(2,1)} %get-tuple-element.25) | copy-start | bytes 884740
  180.2 4.1 %copy-start.3 = (bf16[768,768]{1,0:T(8,128)(2,1)S(1)}, bf16[768,768]{1,0:T(8,128)(2,1)}, u32[]{:S(2)}) copy-start(bf16[768,768]{1,0:T(8,128)(2,1)} %get-tuple-element.26) | copy-start | bytes 3538948
  184.3 2.9 %copy-start.2 = (bf16[768,768]{1,0:T(8,128)(2,1)S(1)}, bf16[768,768]{1,0:T(8,128)(2,1)}, u32[]{:S(2)}) copy-start(bf16[768,768]{1,0:T(8,128)(2,1)} %get-tuple-element.27) | copy-start | bytes 3538948
  187.2 2.1 %copy-start.1 = (bf16[1024,768]{1,0:T(8,128)(2,1)S(1)}, bf16[1024,768]{1,0:T(8,128)(2,1)}, u32[]{:S(2)}) copy-start(bf16[1024,768]{1,0:T(8,128)(2,1)} %get-tuple-element.50) | copy-start | bytes 4718596
  188.8 2.6 %copy-start = (f32[1024,768]{1,0:T(8,128)S(1)}, f32[1024,768]{1,0:T(8,128)}, u32[]{:S(2)}) copy-start(f32[1024,768]{1,0:T(8,128)} %get-tuple-element.51) | copy-start | bytes 9437188

commit v5 on v4

--- a/solution.py
+++ b/solution.py
@@ -282,34 +282,35 @@
 
     for t in (q_in, k_in, v_in):
         ag_near(t)
-    project(y, {0: [run(ag_y, q_in)]})
+    ag_y(q_in)
+    project(y, {0: [run(ag_y, k_in)], 1: [run(ag_y, v_in)]})
     attend(
         y,
         {
-            0: [run(ag_y, k_in)],
-            1: [*near(q_in), run(ag_y, v_in)],
-            4: near(k_in),
-            5: [run(ag_diag, q_in), *near(v_in), run(ag_y, ups[0]), run(ag_y, downs[0]), run(ag_y, o_in)],
+            0: near(q_in),
+            2: near(k_in),
+            3: [*near(v_in), run(ag_y, ups[0]), run(ag_y, downs[0]), run(ag_y, o_in)],
+            4: [run(ag_diag, q_in)],
+            5: [run(ag_diag, k_in)],
         },
     )
-    ag_diag(k_in)
     ag_diag(v_in)
     for t in (q_in, k_in, v_in):
         ag_rest(t)
-    project(1 - y, {1: near(ups[0])})
+    project(1 - y, {0: near(ups[0]), 1: near(downs[0])})
     attend(
         1 - y,
         {
-            1: [*near(downs[0]), run(ag_y, ups[1])],
-            2: [*near(o_in), run(ag_y, downs[1])],
+            0: [run(ag_y, ups[1])],
+            1: [*near(o_in), run(ag_y, downs[1])],
             3: [run(ag_diag, ups[0])],
-            5: [run(ag_diag, downs[0]), *near(ups[1]), run(ag_y, ups[2]), run(ag_y, downs[2])],
+            4: [run(ag_diag, downs[0])],
+            5: [*near(ups[1]), run(ag_diag, o_in)],
         },
     )
     for s in range(sequences):
         stat_rows[s] = hid[rows_of(s, LEN), :128].T
     ag_near(o_in)
-    ag_diag(o_in)
     ag_rest(o_in)
 
     def out_step(i):
@@ -319,7 +320,7 @@
         pltpu.make_async_copy(hid.at[r, :], hidden_hbm.at[r, :], tile_a.at[i]).start()
         normal, _ = normal_of(value)
         n2[r, :] = (normal * vec_recv[0, 5:6, :] + vec_recv[0, 6:7, :]).astype(BF16)
-        at_steps(i, {1: near(downs[1]), 3: [run(ag_diag, ups[1])]})
+        at_steps(i, {0: [run(ag_y, ups[2]), run(ag_y, downs[2])], 2: near(downs[1])})
 
     each(count // TILE, out_step)
     for t in range(o_in + 1, tensors):
@@ -336,17 +337,26 @@
         rows = kept.shape[0]
         return (u, rows, kept, cr, yr, xr)
 
-    def own_half(rows):
-        return ds(xb * (rows // 2), rows // 2, rows // 4)
-
-    def other_half(rows):
-        return ds((1 - xb) * (rows // 2), rows // 2, rows // 4)
-
-    def own_quarter(rows):
-        return ds(xb * (rows // 2) + zb * (rows // 4), rows // 4)
-
-    def other_quarter(rows):
-        return ds(xb * (rows // 2) + (1 - zb) * (rows // 4), rows // 4)
+    level_first = (1,)
+
+    def order_of(unit_of):
+        return (level, side, zb, xb) if unit_of[0] in level_first else (side, level, xb, zb)
+
+    def own_half(unit_of):
+        rows, (_, _, a, _) = unit_of[1], order_of(unit_of)
+        return ds(a * (rows // 2), rows // 2, rows // 4)
+
+    def other_half(unit_of):
+        rows, (_, _, a, _) = unit_of[1], order_of(unit_of)
+        return ds((1 - a) * (rows // 2), rows // 2, rows // 4)
+
+    def own_quarter(unit_of):
+        rows, (_, _, a, b) = unit_of[1], order_of(unit_of)
+        return ds(a * (rows // 2) + b * (rows // 4), rows // 4)
+
+    def other_quarter(unit_of):
+        rows, (_, _, a, b) = unit_of[1], order_of(unit_of)
+        return ds(a * (rows // 2) + (1 - b) * (rows // 4), rows // 4)
 
     def send_unit(u, k, source, target, device):
         remote(source, target, unit_send.at[u, k], unit_recv.at[u, k], device).start()
@@ -356,8 +366,8 @@
         got(cr, unit_recv.at[u, 2])
         got(yr, unit_recv.at[u, 1])
         add_into(kept, cr, yr)
-        pl.semaphore_signal(ready.at[u, 2], inc=1, device_id=level, device_id_type=MESH)
-        send_unit(u, 3, kept.at[other_half(rows), :], xr, side)
+        pl.semaphore_signal(ready.at[u, 2], inc=1, device_id=order_of(unit_of)[1], device_id_type=MESH)
+        send_unit(u, 3, kept.at[other_half(unit_of), :], xr, order_of(unit_of)[0])
 
     def far_room(unit_of, i):
         u, rows, kept, cr, yr, xr = unit_of
@@ -366,7 +376,7 @@
     def send_far(unit_of, i):
         u, rows, kept, cr, yr, xr = unit_of
         pl.semaphore_wait(ready.at[u, 3 + i], 1)
-        send_unit(u, 7 + i, kept.at[own_quarter(rows), :], far_room(unit_of, i), far[i])
+        send_unit(u, 7 + i, kept.at[own_quarter(unit_of), :], far_room(unit_of, i), far[i])
 
     def take_side(unit_of):
         u, rows, kept, cr, yr, xr = unit_of
@@ -374,26 +384,26 @@
             pl.semaphore_signal(ready.at[u, 3 + i], inc=1, device_id=far[i], device_id_type=MESH)
         got(xr, unit_recv.at[u, 3])
         sent(xr, unit_send.at[u, 3])
-        pl.semaphore_signal(ready.at[u, 0], inc=1, device_id=side, device_id_type=MESH)
-        add_into(kept.at[own_half(rows), :], xr)
+        pl.semaphore_signal(ready.at[u, 0], inc=1, device_id=order_of(unit_of)[0], device_id_type=MESH)
+        add_into(kept.at[own_half(unit_of), :], xr)
         pl.semaphore_wait(ready.at[u, 2], 1)
-        send_unit(u, 4, kept.at[other_quarter(rows), :], yr.at[: rows // 4, :], level)
+        send_unit(u, 4, kept.at[other_quarter(unit_of), :], yr.at[: rows // 4, :], order_of(unit_of)[1])
 
     def give_level(unit_of):
         u, rows, kept, cr, yr, xr = unit_of
-        mine = kept.at[own_quarter(rows), :]
+        mine = kept.at[own_quarter(unit_of), :]
         pl.semaphore_wait(ready.at[u, 1], 1)
-        send_unit(u, 5, mine, mine, level)
+        send_unit(u, 5, mine, mine, order_of(unit_of)[1])
         pl.semaphore_wait(ready.at[u, 0], 1)
-        send_unit(u, 6, mine, mine, side)
+        send_unit(u, 6, mine, mine, order_of(unit_of)[0])
 
     def take_level(unit_of):
         u, rows, kept, cr, yr, xr = unit_of
         landed = yr.at[: rows // 4, :]
         got(landed, unit_recv.at[u, 4])
         sent(landed, unit_send.at[u, 4])
-        pl.semaphore_signal(ready.at[u, 1], inc=1, device_id=level, device_id_type=MESH)
-        mine = kept.at[own_quarter(rows), :]
+        pl.semaphore_signal(ready.at[u, 1], inc=1, device_id=order_of(unit_of)[1], device_id_type=MESH)
+        mine = kept.at[own_quarter(unit_of), :]
         add_into(mine, landed)
         if far:
             send_far(unit_of, 0)
@@ -402,7 +412,7 @@
 
     def take_far(unit_of):
         u, rows, kept, cr, yr, xr = unit_of
-        mine = kept.at[own_quarter(rows), :]
+        mine = kept.at[own_quarter(unit_of), :]
         for i, _ in enumerate(far):
             landed = far_room(unit_of, i)
             got(landed, unit_recv.at[u, 7 + i])
@@ -415,14 +425,14 @@
 
     def give_side(unit_of):
         u, rows, kept, cr, yr, xr = unit_of
-        other = kept.at[other_quarter(rows), :]
+        other = kept.at[other_quarter(unit_of), :]
         got(other, unit_recv.at[u, 5])
-        send_unit(u, 7 + rounds_far, other, other, side)
+        send_unit(u, 7 + rounds_far, other, other, order_of(unit_of)[0])
 
     def finish(unit_of, copies):
         u, rows, kept, cr, yr, xr = unit_of
-        got(kept.at[own_quarter(rows), :], unit_recv.at[u, 6])
-        got(kept.at[own_quarter(rows), :], unit_recv.at[u, 7 + rounds_far])
+        got(kept.at[own_quarter(unit_of), :], unit_recv.at[u, 6])
+        got(kept.at[own_quarter(unit_of), :], unit_recv.at[u, 7 + rounds_far])
         for copy in copies():
             copy.start()
 
@@ -438,9 +448,9 @@
 
     def unit_sends(unit_of):
         u, rows, kept, cr, yr, xr = unit_of
-        sent(kept.at[own_half(rows), :] if u == 2 else kept, unit_send.at[u, 1])
+        sent(kept.at[own_half(unit_of), :] if u == 2 else kept, unit_send.at[u, 1])
         for k in (5, 6, 7 + rounds_far):
-            sent(kept.at[own_quarter(rows), :], unit_send.at[u, k])
+            sent(kept.at[own_quarter(unit_of), :], unit_send.at[u, k])
 
     feeds = [
         unit(s, fp.at[feed_slots + 3 + s], fcr.at[s], fyr.at[s], fxr.at[s]) for s in range(3)
@@ -464,16 +474,15 @@
 
         @pl.when(sub == 2)
         def _():
-            rows = fp.shape[1]
-            send_unit(2, 8 + rounds_far, fp.at[slot, other_half(rows), :], fyr.at[2, own_half(rows), :], side)
+            send_unit(2, 8 + rounds_far, fp.at[slot, other_half(feeds[2]), :], fyr.at[2, own_half(feeds[2]), :], order_of(feeds[2])[0])
 
     def last_other():
         _, rows, _, _, yr, _ = feeds[2]
         passed = fp.at[feed_slots + 2]
-        landed = yr.at[other_half(rows), :]
+        landed = yr.at[other_half(feeds[2]), :]
         got(landed, unit_recv.at[2, 8 + rounds_far])
-        add_into(passed.at[own_half(rows), :], landed)
-        send_unit(2, 1, passed.at[own_half(rows), :], yr.at[own_half(rows), :], above)
+        add_into(passed.at[own_half(feeds[2]), :], landed)
+        send_unit(2, 1, passed.at[own_half(feeds[2]), :], yr.at[own_half(feeds[2]), :], above)
 
     def last_sum():
         u, rows, kept, cr, _, xr = feeds[2]
@@ -481,19 +490,19 @@
         add_into(kept, cr)
         for i in range(len(far)):
             pl.semaphore_signal(ready.at[u, 3 + i], inc=1, device_id=far[i], device_id_type=MESH)
-        send_unit(u, 3, kept.at[other_half(rows), :], xr, side)
+        send_unit(u, 3, kept.at[other_half(feeds[2]), :], xr, order_of(feeds[2])[0])
 
     def last_both():
         u, rows, kept, _, yr, xr = feeds[2]
-        mine, landed = kept.at[own_half(rows), :], yr.at[own_half(rows), :]
+        mine, landed = kept.at[own_half(feeds[2]), :], yr.at[own_half(feeds[2]), :]
         got(xr, unit_recv.at[u, 3])
         sent(xr, unit_send.at[u, 3])
-        pl.semaphore_signal(ready.at[u, 0], inc=1, device_id=side, device_id_type=MESH)
+        pl.semaphore_signal(ready.at[u, 0], inc=1, device_id=order_of(feeds[2])[0], device_id_type=MESH)
         got(landed, unit_recv.at[u, 1])
         add_into(mine, xr, landed)
-        pl.semaphore_signal(ready.at[u, 2], inc=1, device_id=level, device_id_type=MESH)
+        pl.semaphore_signal(ready.at[u, 2], inc=1, device_id=order_of(feeds[2])[1], device_id_type=MESH)
         pl.semaphore_wait(ready.at[u, 2], 1)
-        send_unit(u, 4, kept.at[other_quarter(rows), :], yr.at[: rows // 4, :], level)
+        send_unit(u, 4, kept.at[other_quarter(feeds[2]), :], yr.at[: rows // 4, :], order_of(feeds[2])[1])
 
     def feed_third(sub, slot):
         pl.semaphore_wait(credit, 1)
@@ -552,8 +561,8 @@
         at_steps(
             i,
             {
-                0: [*near(ups[2]), run(ag_diag, downs[1])],
-                1: [*near(downs[2]), run(ag_rest, ups[1]), run(ag_rest, downs[1])],
+                0: [run(ag_diag, ups[1]), run(ag_diag, downs[1]), *near(ups[2])],
+                1: [run(ag_rest, ups[1]), run(ag_rest, downs[1]), *near(downs[2])],
                 3: [run(ag_diag, ups[2]), run(ag_diag, downs[2]), run(ag_rest, ups[2]), run(ag_rest, downs[2])],
                 8: [run(take_sum, feeds[0])],
                 9: [last_other],
@@ -659,21 +668,22 @@
         {
             0: [run(small_second, 0), run(small_third, 0), last_both],
             3: [
-                run(weight_of_outer, 1 - y, 0), run(small_first, 1), run(small_first, 2), run(take_level, feeds[2]),
-                run(take_far, feeds[0]), run(take_side, feeds[1]), run(take_sum, proj),
+                run(weight_of_outer, 1 - y, 0), run(small_first, 1), run(small_first, 2), run(take_far, feeds[0]),
+                run(take_sum, proj),
             ],
-            4: [run(small_second, 1), run(small_second, 2)],
+            2: [run(take_side, feeds[1])],
+            4: [run(small_second, 1), run(small_second, 2), run(take_level, feeds[1])],
+            5: [run(take_level, feeds[2])],
         },
     )
     weight_of_shared(1 - y, 0)
     small_first(3)
-    take_side(proj)
     attend_back(
         y,
         {
             0: [run(small_second, 3), run(give_side, feeds[0])],
-            2: [run(take_level, feeds[1])],
-            3: [run(weight_of_outer, y, 1), run(small_third, 1), run(small_third, 2), run(take_far, feeds[2])],
+            1: [run(take_side, proj)],
+            3: [run(weight_of_outer, y, 1), run(small_third, 1), run(small_third, 2), run(take_far, feeds[1])],
             4: [run(take_sum, heads_a), run(take_level, proj)],
             5: [run(take_sum, heads_b)],
         },
@@ -697,9 +707,9 @@
         at_steps(
             i,
             {
-                0: [run(take_side, heads_a)],
-                1: [run(take_sum, shared), run(take_far, feeds[1]), run(give_side, feeds[2])],
-                3: [run(take_side, heads_b), run(take_far, proj)],
+                0: [run(take_far, feeds[2]), run(give_side, feeds[1])],
+                1: [run(take_sum, shared)],
+                2: [run(take_side, heads_a), run(take_far, proj)],
             },
         )
 
@@ -739,9 +749,9 @@
         at_steps(
             i,
             {
-                0: [run(take_level, heads_a), run(vec_step, 0)],
-                1: [run(take_side, shared), run(vec_step, 1)],
-                2: [run(give_side, feeds[1]), run(vec_step, 2)],
+                0: [run(take_side, heads_b), run(give_side, feeds[2]), run(vec_step, 0)],
+                1: [run(vec_step, 1)],
+                2: [run(take_level, heads_a), run(take_side, shared), run(vec_step, 2)],
                 3: [run(take_level, heads_b), run(vec_step, 3)],
             },
         )
@@ -790,7 +800,7 @@
     for n in range(4):
         for k in (0, 2):
             sent(op.at[4 * n + k], unit_send.at[3 + n, k])
-    sent(feeds[2][2].at[own_half(2 * PIECE), :], unit_send.at[2, 8 + rounds_far])
+    sent(feeds[2][2].at[own_half(feeds[2]), :], unit_send.at[2, 8 + rounds_far])
     for unit_of in feeds + smalls:
         unit_sends(unit_of)
     for i in range(count // TILE):

time: 194 us -> 186 us (0.959)
  Pallas kernels: 174 us -> 166 us
    pallas_call x1, Pallas kernels: 174 us -> 166 us  [per_device(): pl.pallas_call(functools.partial(layer_kernel, dp), out_shape=outs, in_sp...]
where the time goes in v5:
time: 186 us
  Pallas kernels  166 us (89%)
  local copies, waits for them, and re-layouts  10.6 us (6%)
  other arithmetic  8.04 us (4%)
    pallas_call x1, Pallas kernels, per_device(): pl.pallas_call(functools.partial(layer_kernel, dp), out_shape=outs, in_sp...  166 us
    unnamed x12, local copies, waits for them, and re-layouts  4.25 us

profile of v5, /device:TPU:0, one launch (start us, length us, event | category | flops | bytes accessed | tf_op | source)
XLA Modules:
  0.0 185.7 jit_solution(12661211168305420244)
XLA Ops:
  0.6 0.8 reshape.46
  1.4 0.8 slice_reduce_fusion.1
  2.2 1.4 fusion.8.small_own
  3.6 1.3 reshape.47.segment
  4.9 166.4 %shard_map.254 = (bf16[1024,768]{1,0:T(8,128)(2,1)}, f32[1024,768]{1,0:T(8,128)}, bf16[768,768]{1,0:T(8,128)(2,1)}, bf16[768,768]{1,0:T(8,128)(2,1)}, bf16[192,7...) custom-call(bf16[12,192]{1,0:T(8,128)(2,1)} %fusion.8.small_own, ...), custom_call_target="tpu_custom_call" | custom-call | tf_op jit(solution)/shard_map/pallas_call | solution.py:872
  171.4 0.0 copy-start.4
  171.4 0.8 slice.32
  172.2 0.7 fusion.16
  172.8 0.0 copy-start.3
  172.8 2.6 %convert_bitcast_fusion = f32[3,768,192]{1,2,0:T(8,128)} fusion(bf16[3,192,768]{2,1,0:T(8,128)(2,1)} %bitcast.12), kind=kLoop, calls=%fused_computation | loop fusion | flops 442368 | bytes 2654208 | tf_op jit(solution)/shard_map/convert_element_type | solution.py:885
  175.4 0.7 dynamic-slice.2
  176.1 0.0 copy-done.4
  176.1 0.9 convert_element_type.23
  176.9 0.0 copy-done.3
  176.9 0.0 copy-start.2
  176.9 1.6 convert_element_type.24
  178.5 1.3 dynamic-slice_reduce_fusion
  179.9 0.0 copy-done.2
  179.9 0.0 copy-start.1
  179.9 1.6 convert_element_type.25
  181.4 0.0 copy-start
  181.4 0.5 copy-done.1
  182.0 1.1 copy.31
  183.1 0.9 copy-done
  184.0 1.7 copy.32
  (1 shorter events, 0.0 us)
Async XLA Ops:
  171.4 4.7 %copy-start.4 = (bf16[192,768]{1,0:T(8,128)(2,1)S(1)}, bf16[192,768]{1,0:T(8,128)(2,1)}, u32[]{:S(2)}) copy-start(bf16[192,768]{1,0:T(8,128)(2,1)} %get-tuple-element.25) | copy-start | bytes 884740
  172.8 4.1 %copy-start.3 = (bf16[768,768]{1,0:T(8,128)(2,1)S(1)}, bf16[768,768]{1,0:T(8,128)(2,1)}, u32[]{:S(2)}) copy-start(bf16[768,768]{1,0:T(8,128)(2,1)} %get-tuple-element.26) | copy-start | bytes 3538948
  176.9 2.9 %copy-start.2 = (bf16[768,768]{1,0:T(8,128)(2,1)S(1)}, bf16[768,768]{1,0:T(8,128)(2,1)}, u32[]{:S(2)}) copy-start(bf16[768,768]{1,0:T(8,128)(2,1)} %get-tuple-element.27) | copy-start | bytes 3538948
  179.9 2.1 %copy-start.1 = (bf16[1024,768]{1,0:T(8,128)(2,1)S(1)}, bf16[1024,768]{1,0:T(8,128)(2,1)}, u32[]{:S(2)}) copy-start(bf16[1024,768]{1,0:T(8,128)(2,1)} %get-tuple-element.50) | copy-start | bytes 4718596
  181.4 2.6 %copy-start = (f32[1024,768]{1,0:T(8,128)S(1)}, f32[1024,768]{1,0:T(8,128)}, u32[]{:S(2)}) copy-start(f32[1024,768]{1,0:T(8,128)} %get-tuple-element.51) | copy-start | bytes 9437188

commit v6 on v5

--- a/solution.py
+++ b/solution.py
@@ -831,8 +831,11 @@
     place = lax.broadcasted_iota(jnp.int32, small_own.shape, 0) * part + lax.broadcasted_iota(
         jnp.int32, small_own.shape, 1
     )
-    for i, piece in reversed(list(enumerate((ln1_gain, ln1_bias, b_qv[0], b_qv[1], b_out, ln2_gain, ln2_bias, b_down)))):
-        small_own = jnp.where(place < (i + 1) * part, piece[None, :], small_own)
+    pieces = [
+        ln1_gain[None], ln1_bias[None], b_qv[:1], b_qv[1:], b_out[None], ln2_gain[None], ln2_bias[None], b_down[None],
+    ]
+    for i, piece in reversed(list(enumerate(pieces))):
+        small_own = jnp.where(place < (i + 1) * part, piece, small_own)
     qkv_own = w_qkv.swapaxes(1, 2)
 
     def shape(*dims, kind=BF16):
@@ -880,7 +883,7 @@
         ),
     )(*args)
     output, grad_x, g_down, g_up, proj, attn, vec = results[:7]
-    eight = lax.dynamic_slice_in_dim(vec[:8], me * part, part, 1)
+    eight = lax.dynamic_slice(vec, (0, me * part), (8, part))
     grad_b_up = lax.dynamic_slice_in_dim(vec, 8 + me, 1, 0).reshape(-1)
     g_qkv = attn.reshape(3, part, width).swapaxes(1, 2).astype(F32)
     return (

time: 186 us -> 187 us (level)
  no operation moved by 1% of the time
where the time goes in v6:
time: 187 us
  Pallas kernels  166 us (89%)
  local copies, waits for them, and re-layouts  11.4 us (6%)
  other arithmetic  8.04 us (4%)
    pallas_call x1, Pallas kernels, per_device(): pl.pallas_call(functools.partial(layer_kernel, dp), out_shape=outs, in_sp...  166 us
    unnamed x12, local copies, waits for them, and re-layouts  4.25 us

profile of v6, /device:TPU:0, one launch (start us, length us, event | category | flops | bytes accessed | tf_op | source)
XLA Modules:
  0.0 186.6 jit_solution(988092275313922433)
XLA Ops:
  0.6 0.8 reshape.46
  1.4 0.8 slice_reduce_fusion.1
  2.2 1.4 fusion.8.small_own
  3.6 1.3 reshape.47.segment
  4.9 166.4 %shard_map.254 = (bf16[1024,768]{1,0:T(8,128)(2,1)}, f32[1024,768]{1,0:T(8,128)}, bf16[768,768]{1,0:T(8,128)(2,1)}, bf16[768,768]{1,0:T(8,128)(2,1)}, bf16[192,7...) custom-call(bf16[12,192]{1,0:T(8,128)(2,1)} %fusion.8.small_own, ...), custom_call_target="tpu_custom_call" | custom-call | tf_op jit(solution)/shard_map/pallas_call | solution.py:875
  171.4 0.0 copy-start.4
  171.4 1.6 fusion.16
  173.0 0.0 copy-start.3
  173.0 2.6 %convert_bitcast_fusion = f32[3,768,192]{1,2,0:T(8,128)} fusion(bf16[3,192,768]{2,1,0:T(8,128)(2,1)} %bitcast.12), kind=kLoop, calls=%fused_computation | loop fusion | flops 442368 | bytes 2654208 | tf_op jit(solution)/shard_map/convert_element_type | solution.py:888
  175.6 1.4 dynamic-slice.2
  176.9 0.0 copy-done.4
  177.0 0.9 convert_element_type.23
  177.8 0.0 copy-done.3
  177.8 0.0 copy-start.2
  177.8 1.6 convert_element_type.24
  179.4 1.3 dynamic-slice_reduce_fusion
  180.7 0.0 copy-done.2
  180.7 0.0 copy-start.1
  180.7 1.6 convert_element_type.25
  182.3 0.0 copy-start
  182.3 0.5 copy-done.1
  182.9 1.1 copy.31
  184.0 0.9 copy-done
  184.9 1.7 copy.32
  (1 shorter events, 0.0 us)
Async XLA Ops:
  171.4 5.6 %copy-start.4 = (bf16[192,768]{1,0:T(8,128)(2,1)S(1)}, bf16[192,768]{1,0:T(8,128)(2,1)}, u32[]{:S(2)}) copy-start(bf16[192,768]{1,0:T(8,128)(2,1)} %get-tuple-element.25) | copy-start | bytes 884740
  173.0 4.8 %copy-start.3 = (bf16[768,768]{1,0:T(8,128)(2,1)S(1)}, bf16[768,768]{1,0:T(8,128)(2,1)}, u32[]{:S(2)}) copy-start(bf16[768,768]{1,0:T(8,128)(2,1)} %get-tuple-element.26) | copy-start | bytes 3538948
  177.8 2.9 %copy-start.2 = (bf16[768,768]{1,0:T(8,128)(2,1)S(1)}, bf16[768,768]{1,0:T(8,128)(2,1)}, u32[]{:S(2)}) copy-start(bf16[768,768]{1,0:T(8,128)(2,1)} %get-tuple-element.27) | copy-start | bytes 3538948
  180.7 2.1 %copy-start.1 = (bf16[1024,768]{1,0:T(8,128)(2,1)S(1)}, bf16[1024,768]{1,0:T(8,128)(2,1)}, u32[]{:S(2)}) copy-start(bf16[1024,768]{1,0:T(8,128)(2,1)} %get-tuple-element.50) | copy-start | bytes 4718596
  182.3 2.6 %copy-start = (f32[1024,768]{1,0:T(8,128)S(1)}, f32[1024,768]{1,0:T(8,128)}, u32[]{:S(2)}) copy-start(f32[1024,768]{1,0:T(8,128)} %get-tuple-element.51) | copy-start | bytes 9437188
